TPU v7x, 512 devices: a whole 4x4x16 slice. The times are simulated.
512 devices in a mesh: tm: 32 (over z, core), space: 16 (over x, y).
Axes of the slice: x: 4, y: 4, z: 16, core: 2. Of those that a mesh axis runs over, the one named last changes fastest.
Arguments:
- sections: int32 [32], replicated, may hold values from 1 to 4, 80 in all
- right_side: bfloat16 [128, 64, 2048], P('tm'), may hold values from -6 to 6
- tip_side: float32 [64, 8], replicated, may hold values from -48 to 48
- diag_inverse: bfloat16 [128, 2048, 2048], P('tm', 'space'), may hold values from -0.08 to 0.42, as said below
- forward_coupling: bfloat16 [128, 2048, 128], P('tm', 'space'), may hold values from -1 to 1
- backward_coupling: bfloat16 [128, 2048, 128], P('tm', 'space'), may hold values from -1 to 1
- arrow_rows: bfloat16 [128, 8, 2048], P('tm', None, 'space'), may hold values from -3.3 to 3.3
- tip_inverse: float32 [8, 8], replicated, may hold values from -0.4 to 0.4, as said below
Outputs:
- solution: float32 [128, 64, 2048], P('tm', None, 'space')
- tip_solution: float32 [64, 8], replicated
Inputs may be any that keep to these rules, and one draw needn't show every extreme that they name: Section i holds the live slots i * 4 to i * 4 + sections[i] - 1. `diag_inverse`: each block is lower triangular with a positive diagonal. `tip_inverse`: lower triangular with a positive diagonal.
All inputs are finite; a program needn't handle non-finite values.
Results may differ from a plain program's by a relative error of at most 0.0031.
Values sent between devices are 32-bit elements; how exact they have to be, the bound alone decides.
No kernel may reach another device: no remote copies, remote signals or barrier semaphores. Data moves between devices by JAX's collectives and lax.ppermute only.
A program may use at most 64 MiB of HBM per device.

v0:
```python
import functools

import jax
import jax.numpy as jnp
from jax import lax
from jax.sharding import Mesh
from jax.sharding import PartitionSpec as P

TM = ("tm_0", "tm_1")
TM_SPACE = ("tm_0", "tm_1", "space_0", "space_1")
SPACE = ("space_0", "space_1")


def filled_with(shard, identity):
    return jax.tree.map(
        lambda a, e: jnp.broadcast_to(jnp.asarray(e, a.dtype), a.shape), shard, identity
    )


def carried_in(shard, axes, combine, identity, reverse):
    before = start = filled_with(shard, identity)
    running = shard
    for axis in reversed(axes):
        length, place = (lax.axis_size(axis), lax.axis_index(axis))
        pieces = jax.tree.map(lambda part: lax.all_gather(part, axis), running)
        inside, running = (start, start)
        for k in reversed(range(length)) if reverse else range(length):
            passed = k > place if reverse else k < place
            running = combine(running, jax.tree.map(lambda part: part[k], pieces))
            inside = jax.tree.map(lambda new, old: jnp.where(passed, new, old), running, inside)
        before = combine(inside, before)
    return before


def by_axis(shard, axes):
    return functools.reduce(lax.psum, axes, shard)


def cut_along(shard, dim, length):
    before, after = (shard.shape[:dim], shard.shape[dim + 1 :])
    return jnp.moveaxis(shard.reshape(*before, length, -1, *after), dim, 0)


def summed_on_arrival(shard, axis, dim):
    length = lax.axis_size(axis)
    blocks = lax.all_to_all(cut_along(shard, dim, length), axis, 0, 0, tiled=True)
    return jnp.sum(blocks, axis=0)


def couple(states, coupling):
    row_count, node_width = states.shape
    sub_width = coupling.shape[1]
    sub_count = node_width // sub_width
    shaped = states.reshape(row_count, sub_count, sub_width)
    blocks = coupling.astype(jnp.float32).reshape(sub_count, sub_width, sub_width)
    return jnp.einsum("rnk,nik->rni", shaped, blocks, precision=lax.Precision.HIGHEST).reshape(
        row_count, node_width
    )


def apply_map(offset, mapping):
    row_count, node_width = offset.shape
    sub_count, sub_width = (mapping.shape[0], mapping.shape[1])
    shaped = offset.reshape(row_count, sub_count, sub_width)
    return jnp.einsum("rni,nik->rnk", shaped, mapping, precision=lax.Precision.HIGHEST).reshape(
        row_count, node_width
    )


def compose(earlier, later):
    mapping = jnp.einsum("nij,njk->nik", earlier[0], later[0], precision=lax.Precision.HIGHEST)
    return (mapping, apply_map(earlier[1], later[0]) + later[1])


def section_map(driven, couplings, live_count, order):
    row_count, node_width = (driven.shape[1], driven.shape[2])
    sub_width = couplings.shape[2]
    sub_count = node_width // sub_width
    mapping = jnp.broadcast_to(
        jnp.eye(sub_width, dtype=jnp.float32), (sub_count, sub_width, sub_width)
    )
    offset = jnp.zeros((row_count, node_width), jnp.float32)
    for slot_index in order:
        blocks = couplings[slot_index].astype(jnp.float32).reshape(sub_count, sub_width, sub_width)
        new_offset = driven[slot_index] - couple(offset, couplings[slot_index])
        new_mapping = -jnp.einsum("nij,nkj->nik", mapping, blocks, precision=lax.Precision.HIGHEST)
        live_flag = slot_index < live_count
        offset = jnp.where(live_flag, new_offset, offset)
        mapping = jnp.where(live_flag, new_mapping, mapping)
    return (mapping, offset)


def resolve(incoming, driven, couplings, live_count, order):
    outputs = [None] * driven.shape[0]
    previous = incoming
    for slot_index in order:
        update = driven[slot_index] - couple(previous, couplings[slot_index])
        live_flag = slot_index < live_count
        outputs[slot_index] = jnp.where(live_flag, update, jnp.float32(0.0))
        previous = jnp.where(live_flag, update, previous)
    return jnp.stack(outputs, 0)


def on_device(
    sections,
    right_side,
    tip_side,
    diag_inverse,
    forward_coupling,
    backward_coupling,
    arrow_rows,
    tip_inverse,
):
    slot_count = diag_inverse.shape[0]
    position = lax.axis_index(TM)
    section_len = lax.dynamic_index_in_dim(sections, position, 0, keepdims=False)
    forward_order = list(range(slot_count))
    backward_order = list(reversed(range(slot_count)))
    driven = jnp.einsum(
        "trs,tqs->trq", right_side, diag_inverse, preferred_element_type=jnp.float32
    )
    forward_pair = section_map(driven, forward_coupling, section_len, forward_order)
    identity = (
        jnp.broadcast_to(
            jnp.eye(forward_pair[0].shape[1], dtype=jnp.float32), forward_pair[0].shape
        ),
        jnp.zeros_like(forward_pair[1]),
    )
    forward_in = carried_in(forward_pair, TM, compose, identity, False)[1]
    forward_states = resolve(forward_in, driven, forward_coupling, section_len, forward_order)
    partial_value = jnp.einsum(
        "trq,tfq->rf",
        forward_states.astype(jnp.bfloat16),
        arrow_rows,
        preferred_element_type=jnp.float32,
    )
    arrow_total = by_axis(partial_value, TM_SPACE)
    tip_state = jnp.dot(tip_side - arrow_total, tip_inverse.T, precision=lax.Precision.HIGHEST)
    tip_solution = jnp.dot(tip_state, tip_inverse, precision=lax.Precision.HIGHEST)
    arrow_wide = arrow_rows.astype(jnp.float32)
    backward_source = (
        forward_states
        - jnp.einsum("rf,tfq->trq", tip_solution, arrow_wide, precision=lax.Precision.HIGHEST)
    ).astype(jnp.bfloat16)
    source_terms = jnp.einsum(
        "trq,tqs->trs", backward_source, diag_inverse, preferred_element_type=jnp.float32
    )
    sources = summed_on_arrival(source_terms, SPACE, 2)
    backward_pair = section_map(sources, backward_coupling, section_len, backward_order)
    backward_in = carried_in(backward_pair, TM, compose, identity, True)[1]
    solution = resolve(backward_in, sources, backward_coupling, section_len, backward_order)
    return (solution, tip_solution)


def solution(mesh):
    torus = Mesh(mesh.devices.reshape(16, 2, 4, 4), ("tm_0", "tm_1", "space_0", "space_1"))
    return jax.shard_map(
        on_device,
        mesh=torus,
        in_specs=(
            P(),
            P(TM, None, None),
            P(),
            P(TM, SPACE, None),
            P(TM, SPACE, None),
            P(TM, SPACE, None),
            P(TM, None, SPACE),
            P(),
        ),
        out_specs=(P(TM, None, SPACE), P()),
        check_vma=False,
    )
```

profile of v0, /device:TPU:16, one launch (start us, length us, event | category | flops | bytes accessed | tf_op | source)
XLA Modules:
  0.0 268.3 jit_solution(14216348533339582371)
XLA Ops:
  7.2 1.4 dynamic_slice.4
  14.1 1.0 fusion.6
  15.1 1.9 all-gather
  19.1 2.1 fusion.318
  21.8 1.9 all_gather.44
  24.2 38.5 %all_gather.45 = f32[16,64,128]{2,1,0:T(8,128)S(1)} all-gather(f32[1,64,128]{2,1,0:T(8,128)S(1)} %get-tuple-element.8), channel_id=1, replica_groups=mesh['tm_0'=16,'tm_1'=2,'space_0'=4,'space_1'=4] {'tm_0'}, dimensions={0}, use_global_device_ids=true | all-gather | bytes 557056 | tf_op jit(solution)/shard_map/all_gather | solution.py:25
  62.7 30.8 %all-gather.7.cloned.1.call-done = f32[2048,128]{1,0:T(8,128)} async-done(((f32[128,128]{1,0:T(8,128)}), f32[2048,128]{1,0:T(8,128)}) %all-gather.7.cloned.1.call-update) | async-done | bytes 1048592 | tf_op jit(solution)/shard_map/all_gather | solution.py:25
  94.5 1.0 fusion.51
  95.6 1.0 fusion.50
  96.6 1.0 fusion.49
  97.6 1.0 fusion.48
  98.7 1.0 fusion.47
  99.7 1.0 fusion.46
  100.7 1.0 fusion.45
  101.8 1.0 fusion.44
  102.8 1.0 fusion.43
  103.8 1.0 fusion.42
  104.8 1.0 fusion.41
  105.9 1.0 fusion.40
  106.9 1.0 fusion.39
  107.9 1.0 fusion.38
  109.0 1.1 fusion.37
  111.4 29.2 %psum.28 = f32[64,8]{0,1:T(8,128)S(1)} all-reduce(f32[64,8]{0,1:T(8,128)S(1)} %convolution_bitcast_fusion.40), channel_id=1, replica_groups=mesh['tm_0'=16,'tm_1'=2,'space_0'=4,'space_1'=4] {'tm_0'}, use_global_device_ids=true, to_apply=%region_0.1 | all-reduce | flops 512 | bytes 4096 | tf_op jit(solution)/shard_map/psum | solution.py:36
  140.6 2.5 psum.29
  143.1 10.4 %psum.30 = f32[64,8]{0,1:T(8,128)S(1)} all-reduce(f32[64,8]{0,1:T(8,128)S(1)} %psum.29), channel_id=1, replica_groups=mesh['tm_0'=16,'tm_1'=2,'space_0'=4,'space_1'=4] {'space_0'}, use_global_device_ids=true, to_apply=%region_2.3 | all-reduce | flops 512 | bytes 4096 | tf_op jit(solution)/shard_map/psum | solution.py:36
  153.5 8.3 %psum.31 = f32[64,8]{0,1:T(8,128)S(1)} all-reduce(f32[64,8]{0,1:T(8,128)S(1)} %psum.30), channel_id=1, replica_groups=mesh['tm_0'=16,'tm_1'=2,'space_0'=4,'space_1'=4] {'space_1'}, use_global_device_ids=true, to_apply=%region_3.4 | all-reduce | flops 512 | bytes 4096 | tf_op jit(solution)/shard_map/psum | solution.py:36
  163.0 1.6 copy.13
  164.6 7.0 %all-to-all-start = ((f32[16,4,64,128]{3,2,1,0:T(8,128)}), f32[16,4,64,128]{3,2,1,0:T(8,128)}, u32[]{:S(2)}, u32[]{:S(2)}) async-start(f32[16,4,64,128]{3,2,1,0:T(8,128)} %bitcast.977), calls=%async_computation | async-start | bytes 4194304 | tf_op jit(solution)/shard_map/all_to_all | solution.py:46
  172.4 1.9 all-gather.2
  175.8 20.3 %all-to-all-done = f32[16,4,64,128]{3,2,1,0:T(8,128)} async-done(((f32[16,4,64,128]{3,2,1,0:T(8,128)}), f32[16,4,64,128]{3,2,1,0:T(8,128)}, u32[]{:S(2)}, u32[]{:S(2)}) %all-to-all-start) | async-done | bytes 2097184 | tf_op jit(solution)/shard_map/all_to_all | solution.py:46
  196.1 1.7 reduce_sum.9
  198.5 1.9 all_gather.50
  200.7 29.1 %all_gather.51 = f32[16,64,128]{2,1,0:T(8,128)S(1)} all-gather(f32[1,64,128]{2,1,0:T(8,128)S(1)} %get-tuple-element.15), channel_id=1, replica_groups=mesh['tm_0'=16,'tm_1'=2,'space_0'=4,'space_1'=4] {'tm_0'}, dimensions={0}, use_global_device_ids=true | all-gather | bytes 557056 | tf_op jit(solution)/shard_map/all_gather | solution.py:25
  229.8 13.2 %all-gather.9.cloned.1.call-done = f32[2048,128]{1,0:T(8,128)} async-done(((f32[128,128]{1,0:T(8,128)}), f32[2048,128]{1,0:T(8,128)}) %all-gather.9.cloned.1.call-update) | async-done | bytes 1048592 | tf_op jit(solution)/shard_map/all_gather | solution.py:25
  244.0 1.0 fusion.28
  245.1 1.0 fusion.27
  246.1 1.0 fusion.26
  247.1 1.0 fusion.25
  248.2 1.0 fusion.24
  249.2 1.0 fusion.23
  250.2 1.0 fusion.22
  251.3 1.0 fusion.21
  252.3 1.0 fusion.20
  253.3 1.0 fusion.19
  254.4 1.0 fusion.18
  255.4 1.0 fusion.17
  256.4 1.0 fusion.16
  258.5 1.1 fusion.14
  (66 shorter events, 16.5 us)
Async XLA Ops:
  7.2 11.9 %copy-start = (bf16[4,128,2048]{2,1,0:T(8,128)(2,1)S(1)}, bf16[4,128,2048]{2,1,0:T(8,128)(2,1)}, u32[]{:S(2)}) copy-start(bf16[4,128,2048]{2,1,0:T(8,128)(2,1)} %param.11) | copy-start | bytes 6291460
  7.2 86.3 %all-gather.7.cloned.1.call-start = ((), (), s32[]{:S(2)}) async-start(), calls=%async_computation.1 | async-start | bytes 1114112 | tf_op jit(solution)/shard_map/all_gather | solution.py:25
  14.1 7.1 %copy-start.1 = (bf16[4,128,128]{2,1,0:T(8,128)(2,1)S(1)}, bf16[4,128,128]{2,1,0:T(8,128)(2,1)}, u32[]{:S(2)}) copy-start(bf16[4,128,128]{2,1,0:T(8,128)(2,1)} %param.12) | copy-start | bytes 393220
  19.1 5.0 %copy-start.3 = (f32[128,128]{1,0:T(8,128)S(1)}, f32[128,128]{1,0:T(8,128)}, u32[]{:S(2)}) copy-start(f32[128,128]{1,0:T(8,128)} %fusion.104) | copy-start | bytes 196612
  62.7 48.5 %copy-start.7 = (bf16[4,8,128]{2,1,0:T(8,128)(2,1)S(1)}, bf16[4,8,128]{2,1,0:T(8,128)(2,1)}, u32[]{:S(2)}) copy-start(bf16[4,8,128]{2,1,0:T(8,128)(2,1)} %param.14) | copy-start | bytes 24580
  95.5 66.3 %copy-start.4 = (f32[8,8]{1,0:T(8,128)S(1)}, f32[8,8]{1,0:T(8,128)}, u32[]{:S(2)}) copy-start(f32[8,8]{1,0:T(8,128)} %param.15) | copy-start | bytes 772
  95.6 66.3 %copy-start.6 = (f32[64,8]{0,1:T(8,128)S(1)}, f32[64,8]{0,1:T(8,128)}, u32[]{:S(2)}) copy-start(f32[64,8]{0,1:T(8,128)} %param.10) | copy-start | bytes 6148
  162.2 0.7 copy-start.5
  164.6 7.0 %copy-start.2 = (bf16[4,128,128]{2,1,0:T(8,128)(2,1)S(1)}, bf16[4,128,128]{2,1,0:T(8,128)(2,1)}, u32[]{:S(2)}) copy-start(bf16[4,128,128]{2,1,0:T(8,128)(2,1)} %param.13) | copy-start | bytes 393220
  164.6 31.5 %all-to-all-start = ((f32[16,4,64,128]{3,2,1,0:T(8,128)}), f32[16,4,64,128]{3,2,1,0:T(8,128)}, u32[]{:S(2)}, u32[]{:S(2)}) async-start(f32[16,4,64,128]{3,2,1,0:T(8,128)} %bitcast.977), calls=%async_computation | async-start | bytes 4194304 | tf_op jit(solution)/shard_map/all_to_all | solution.py:46
  171.6 71.5 %all-gather.9.cloned.1.call-start = ((), (), s32[]{:S(2)}) async-start(), calls=%async_computation.2 | async-start | bytes 1114112 | tf_op jit(solution)/shard_map/all_gather | solution.py:25
Sparse Core Ops, SparseCore 0:
  18.2 75.2 all-gather.6
  175.5 67.4 all-gather.8
where the time goes:
time: 270 us; the launch traced here: 268 us
  blocking collectives  126 us (47%)
  waiting for transfers between devices  64.3 us (24%)
  matrix products  48.6 us (18%)
  between operations  17.4 us (6%)
  starting transfers between devices  7.05 us (3%)
  local copies, waits for them, and re-layouts  3.02 us (1%)
    all_gather x6, blocking collectives, carried_in(): pieces = jax.tree.map(lambda part: lax.all_gather(part, axis), running)  75.1 us
    psum x4, blocking collectives, by_axis(): return functools.reduce(lax.psum, axes, shard)  50.4 us
    all_gather x2, waiting for transfers between devices, carried_in(): pieces = jax.tree.map(lambda part: lax.all_gather(part, axis), running)  44 us
    dot_general x40, matrix products, apply_map(): jnp.einsum('rni,nik->rnk', shaped, mapping, precision=lax.Precision.HIGHEST)  34.3 us
    all_to_all x1, waiting for transfers between devices, summed_on_arrival(): lax.all_to_all(cut_along(shard, dim, length), axis, 0, 0, tiled=True)  20.3 us
    all_to_all x1, starting transfers between devices, summed_on_arrival(): lax.all_to_all(cut_along(shard, dim, length), axis, 0, 0, tiled=True)  6.97 us
  transfers between devices with their start and end apart: 3, of which 3 were waited for; matrix products, arithmetic and copies ran while one was open for 3% of the time, Pallas kernels for 0%

commit v1 on v0

v1 whole, which is shorter than its diff:
```python
import functools

import jax
import jax.numpy as jnp
from jax import lax
from jax.experimental import pallas as pl
from jax.experimental.pallas import tpu as pltpu
from jax.sharding import Mesh
from jax.sharding import PartitionSpec as P

F32 = jnp.float32
BF16 = jnp.bfloat16
TM = ("za", "zb", "core")
SPACE = ("x", "y")
T = 4
R = 64
F = 8
W = 128
N = 16
G = R + F
HI = lax.Precision.HIGHEST


def split(x):
    high = x.astype(BF16)
    return high, (x - high.astype(F32)).astype(BF16)


def dot(a, b, dims):
    return lax.dot_general(a, b, ((dims[:1], dims[1:]), ((), ())), preferred_element_type=F32)


def times(x, m):
    xh, xl = split(x)
    mh, ml = split(m)
    return dot(jnp.concatenate([xh, xl, xh], 1), jnp.concatenate([mh, mh, ml], 0), (1, 0))


def times_t(x, c):
    xh, xl = split(x)
    return dot(jnp.concatenate([xh, xl], 1), jnp.concatenate([c, c], 1), (1, 1))


def eye(dtype):
    rows = lax.broadcasted_iota(jnp.int32, (W, W), 0)
    cols = lax.broadcasted_iota(jnp.int32, (W, W), 1)
    return jnp.where(rows == cols, 1.0, 0.0).astype(dtype)


def place():
    return tuple(lax.axis_index(name) for name in TM)


def live_count(sections):
    za, zb, core = place()
    return sections[(za * 4 + zb) * 2 + core]


def join(first, then):
    out = times(first, then[R : R + W])
    return jnp.concatenate([out[:R] + then[:R], out[R:]], 0)


def local_kernel(sections, side, inverse, forward, backward, states, maps, chunk):
    live = live_count(sections)
    state = None
    for t in range(T):
        driven = dot(side[t], inverse[t], (1, 1))
        if t == 0:
            state = jnp.concatenate([driven, -dot(eye(BF16), forward[0], (1, 1))], 0)
        else:
            moved = times_t(state, forward[t])
            state = jnp.where(
                t < live, jnp.concatenate([driven - moved[:R], -moved[R:]], 0), state
            )
        states[t] = state
    chunk[: R + W] = state
    mapping = eye(F32)
    for t in reversed(range(T)):
        mapping = jnp.where(t < live, -times_t(mapping, backward[t]), mapping)
        maps[t] = mapping
    chunk[R + W :] = mapping


def pair_kernel(own, other, out):
    _, _, core = place()
    first = jnp.where(core == 0, own[...], other[...])
    then = jnp.where(core == 0, other[...], own[...])
    both = join(first[: R + W], then[: R + W])
    back = times(then[R + W :], first[R + W :])
    for j in range(4):
        out[j, : R + W] = both
        out[j, R + W :] = back


def group_kernel(got, out, before, after):
    za, zb, _ = place()
    total = got[0, : R + W]
    before[...] = jnp.concatenate([jnp.zeros((R, W), F32), eye(F32)], 0)
    for j in range(1, 4):
        before[...] = jnp.where(zb == j, total, before[...])
        total = join(total, got[j, : R + W])
    back = got[3, R + W :]
    after[...] = eye(F32)
    for j in reversed(range(3)):
        after[...] = jnp.where(zb == j, back, after[...])
        back = times(back, got[j, R + W :])
    back = jnp.concatenate([back, jnp.zeros((R, W), F32)], 0)
    for j in range(4):
        out[j] = jnp.where(j > za, total, back)


def source_kernel(sections, got, before, other, states, inverse, arrow, out):
    za, _, core = place()
    live = live_count(sections)
    entry = jnp.where(za > 0, got[0, :R], 0.0)
    for j in range(1, 3):
        entry = jnp.where(j < za, times(entry, got[j, R:]) + got[j, :R], entry)
    entry = times(entry, before[R:]) + before[:R]
    entry = jnp.where(core == 1, times(entry, other[R : R + W]) + other[:R], entry)
    total = jnp.zeros((F, W), F32)
    pad = jnp.zeros((W - R, W), BF16)
    for t in range(T):
        state = states[t]
        state = jnp.where(t < live, state[:R] + times(entry, state[R:]), 0.0)
        high, low = split(state)
        total += dot(arrow[t], jnp.concatenate([high, pad], 0), (1, 1))
        rows = jnp.concatenate([high, low, arrow[t], jnp.zeros((F, W), BF16)], 0)
        terms = dot(rows, inverse[t], (1, 0))
        for n in range(N):
            cols = slice(n * W, (n + 1) * W)
            out[n, t * G : t * G + R] = terms[:R, cols] + terms[R : 2 * R, cols]
            out[n, t * G + R : (t + 1) * G] = terms[2 * R : 2 * R + F, cols]
    for n in range(N):
        out[n, T * G :] = total


def arrive_kernel(sections, got, backward, sums, chunk):
    live = live_count(sections)
    whole = got[0]
    for n in range(1, N):
        whole = whole + got[n]
    state = jnp.zeros((G, W), F32)
    for t in reversed(range(T)):
        source = whole[t * G : (t + 1) * G]
        state = jnp.where(t < live, source - times_t(state, backward[t]), state)
        sums[t] = state
    chunk[:G] = state
    chunk[G:] = whole[T * G :]


def back_pair_kernel(own, other, chunk, other_chunk, out):
    _, _, core = place()
    first = jnp.where(core == 0, own[...], other[...])
    then = jnp.where(core == 0, other[...], own[...])
    mapping = jnp.where(core == 0, chunk[R + W :], other_chunk[R + W :])
    state = times(then[:G], mapping) + first[:G]
    for j in range(4):
        out[j, :G] = state
        out[j, G:] = own[G:] + other[G:]


def back_group_kernel(got, maps, out, after):
    _, zb, _ = place()
    total = got[3, :G]
    after[...] = jnp.zeros((G, W), F32)
    for j in reversed(range(3)):
        after[...] = jnp.where(zb == j, total, after[...])
        total = times(total, maps[j, R + W :]) + got[j, :G]
    whole = ((got[0, G:] + got[1, G:]) + got[2, G:]) + got[3, G:]
    for j in range(4):
        out[j, :G] = total
        out[j, G:] = whole


def final_kernel(
    sections, got, totals, after, after_map, other, other_chunk, sums, maps, side, tip_inverse, out, tip_out
):
    za, _, core = place()
    live = live_count(sections)
    whole = ((got[0, G:] + got[1, G:]) + got[2, G:]) + got[3, G:]
    gap = side[...] - whole[:, :R]
    tip = lax.dot_general(
        tip_inverse[...], gap, (((1,), (0,)), ((), ())), precision=HI, preferred_element_type=F32
    )
    tip = lax.dot_general(
        tip_inverse[...], tip, (((0,), (0,)), ((), ())), precision=HI, preferred_element_type=F32
    )
    tip_out[...] = tip
    entry = jnp.where(za < 3, got[3, :G], 0.0)
    for j in (2, 1):
        entry = jnp.where(j > za, times(entry, totals[j, :W]) + got[j, :G], entry)
    entry = times(entry, after_map[...]) + after[...]
    entry = jnp.where(core == 0, times(entry, other_chunk[R + W :]) + other[:G], entry)
    tip_high, tip_low = split(tip)
    weights = jnp.concatenate(
        [tip_high.astype(F32), tip_low.astype(F32), tip_high.astype(F32)], 0
    ).astype(BF16)
    for t in range(T):
        state = sums[t] + times(entry, maps[t])
        high, low = split(state[R:])
        parts = jnp.concatenate([high.astype(F32), high.astype(F32), low.astype(F32)], 0).astype(BF16)
        out[t] = jnp.where(t < live, state[:R] - dot(weights, parts, (0, 0)), 0.0)


VMEM = pl.BlockSpec(memory_space=pltpu.VMEM)
SMEM = pl.BlockSpec(memory_space=pltpu.SMEM)


def call(kernel, shapes, *args):
    specs = [SMEM if a.dtype == jnp.int32 else VMEM for a in args]
    shapes = [jax.ShapeDtypeStruct(s, F32) for s in shapes]
    return pl.pallas_call(
        kernel,
        out_shape=shapes,
        in_specs=specs,
        out_specs=[VMEM] * len(shapes),
        name=kernel.__name__,
    )(*args)


def swap(a):
    return lax.ppermute(a, "core", [(0, 1), (1, 0)])


def exchange(a, axis):
    return lax.all_to_all(a, axis, 0, 0, tiled=True)


def on_device(
    sections, right_side, tip_side, diag_inverse, forward_coupling, backward_coupling, arrow_rows, tip_inverse
):
    states, maps, chunk = call(
        local_kernel,
        [(T, R + W, W), (T, W, W), (R + 2 * W, W)],
        sections,
        right_side,
        diag_inverse,
        forward_coupling,
        backward_coupling,
    )
    other_chunk = swap(chunk)
    (out,) = call(pair_kernel, [(4, R + 2 * W, W)], chunk, other_chunk)
    in_group = exchange(out, "zb")
    out, before, after_map = call(group_kernel, [(4, R + W, W), (R + W, W), (W, W)], in_group)
    totals = exchange(out, "za")
    (out,) = call(
        source_kernel,
        [(N, T * G + F, W)],
        sections,
        totals,
        before,
        other_chunk,
        states,
        diag_inverse,
        arrow_rows,
    )
    got = exchange(out, SPACE)
    sums, back_chunk = call(
        arrive_kernel, [(T, G, W), (G + F, W)], sections, got, backward_coupling
    )
    other_back = swap(back_chunk)
    (out,) = call(back_pair_kernel, [(4, G + F, W)], back_chunk, other_back, chunk, other_chunk)
    got = exchange(out, "zb")
    out, after = call(back_group_kernel, [(4, G + F, W), (G, W)], got, in_group)
    got = exchange(out, "za")
    solved, tip = call(
        final_kernel,
        [(T, R, W), (F, R)],
        sections,
        got,
        totals,
        after,
        after_map,
        other_back,
        other_chunk,
        sums,
        maps,
        tip_side.T,
        tip_inverse,
    )
    return solved, tip.T


def solution(mesh):
    torus = Mesh(mesh.devices.reshape(4, 4, 2, 4, 4), TM + SPACE)
    return jax.shard_map(
        on_device,
        mesh=torus,
        in_specs=(
            P(),
            P(TM, None, None),
            P(),
            P(TM, SPACE, None),
            P(TM, SPACE, None),
            P(TM, SPACE, None),
            P(TM, None, SPACE),
            P(),
        ),
        out_specs=(P(TM, None, SPACE), P()),
        check_vma=False,
    )
```

time: 270 us -> 165 us (0.61)
  the two profiles are of different devices: /device:TPU:16 before, /device:TPU:1 now
where the time goes in v1:
time: 165 us; the launch traced here: 161 us
  blocking collectives  118 us (72%)
  Pallas kernels  24.3 us (15%)
  starting transfers between devices  15.2 us (9%)
  waiting for transfers between devices  2.28 us (1%)
    all_to_all x5, blocking collectives, exchange(): return lax.all_to_all(a, axis, 0, 0, tiled=True)  118 us
    pallas_call x8, Pallas kernels, call(): pl.pallas_call(kernel, out_shape=shapes, in_specs=specs, out_specs=[VMEM]...  24.3 us
    ppermute x2, starting transfers between devices, swap(): return lax.ppermute(a, 'core', [(0, 1), (1, 0)])  15.2 us
  transfers between devices with their start and end apart: 2, of which 2 were waited for; matrix products, arithmetic and copies ran while one was open for 0% of the time, Pallas kernels for 0%

profile of v1, /device:TPU:1, one launch (start us, length us, event | category | flops | bytes accessed | tf_op | source)
XLA Modules:
  0.0 161.4 jit_solution(12423747772823675269)
XLA Ops:
  0.6 4.1 %local_kernel.1 = (f32[4,192,128]{2,1,0:T(8,128)}, f32[4,128,128]{2,1,0:T(8,128)}, f32[320,128]{1,0:T(8,128)}) custom-call(s32[32]{0:T(128)} %sections.7, bf16[4,64,2048]{2,1,0:T(8,128)(2,1)} %side.1, bf16[4,128,2048]{2,1,0:T(8,128)(2,1)} %inverse.3, bf16[4,128,128]{2,1,0:T(8,128)(2,1)} %forward.1, bf16[4,128,128]{2,1,0:T(8,128)(2,1)} %backward.3), custom_call_target="tpu_custom_call" | custom-call | tf_op jit(solution)/shard_map/local_kernel/pallas_call | solution.py:213
  4.7 8.7 %collective-permute-start = (f32[320,128]{1,0:T(8,128)}, f32[320,128]{1,0:T(8,128)S(1)}, u32[]{:S(2)}, u32[]{:S(2)}) collective-permute-start(f32[320,128]{1,0:T(8,128)} %get-tuple-element.14.own.chunk), channel_id=1, source_target_pairs={{0,16},{16,0},{1,17},{17,1},{2,18},{18,2},{3,19},{19,3},{4,20},{20... | collective-permute-start | bytes 491528 | tf_op jit(solution)/shard_map/ppermute | solution.py:223
  13.5 1.2 collective-permute-done.other.other_chunk
  14.7 0.0 copy-start
  14.7 0.7 copy-done
  15.3 2.1 %pair_kernel.1 = f32[4,320,128]{2,1,0:T(8,128)} custom-call(f32[320,128]{1,0:T(8,128)} %get-tuple-element.14.own.chunk, f32[320,128]{1,0:T(8,128)} %copy-done), custom_call_target="tpu_custom_call" | custom-call | tf_op jit(solution)/shard_map/pair_kernel/pallas_call | solution.py:213
  17.4 21.3 %all_to_all.25.got.maps = f32[4,320,128]{2,1,0:T(8,128)} all-to-all(f32[4,320,128]{2,1,0:T(8,128)} %pair_kernel.1), channel_id=1, replica_groups=mesh['za'=4,'zb'=4,'core'=2,'x'=4,'y'=4] {'zb'}, dimensions={0} | all-to-all | bytes 1310720 | tf_op jit(solution)/shard_map/all_to_all | solution.py:227
  38.7 2.6 %group_kernel.1 = (f32[4,192,128]{2,1,0:T(8,128)}, f32[192,128]{1,0:T(8,128)}, f32[128,128]{1,0:T(8,128)}) custom-call(f32[4,320,128]{2,1,0:T(8,128)} %all_to_all.25.got.maps), custom_call_target="tpu_custom_call" | custom-call | tf_op jit(solution)/shard_map/group_kernel/pallas_call | solution.py:213
  41.3 31.0 %all_to_all.26.got.totals = f32[4,192,128]{2,1,0:T(8,128)} all-to-all(f32[4,192,128]{2,1,0:T(8,128)} %get-tuple-element.15), channel_id=1, replica_groups=mesh['za'=4,'zb'=4,'core'=2,'x'=4,'y'=4] {'za'}, dimensions={0} | all-to-all | bytes 786432 | tf_op jit(solution)/shard_map/all_to_all | solution.py:227
  72.3 5.3 %source_kernel.1 = f32[16,296,128]{2,1,0:T(8,128)} custom-call(s32[32]{0:T(128)} %sections.7, f32[4,192,128]{2,1,0:T(8,128)} %all_to_all.26.got.totals, f32[192,128]{1,0:T(8,128)} %get-tuple-element.16.before, f32[320,128]{1,0:T(8,128)} %copy-done, f32[4,192,128]{2,1,0:T(8,128)} %get-tuple-element.17.states, bf16[4,128,2048]{2,1,0:T(8,128)(2,1)} %inverse.3, ...), custom_call_target="tpu_custom_call" | custom-call | tf_op jit(solution)/shard_map/source_kernel/pallas_call | solution.py:213
  77.6 34.9 %all_to_all.27.got = f32[16,296,128]{2,1,0:T(8,128)} all-to-all(f32[16,296,128]{2,1,0:T(8,128)} %source_kernel.1), channel_id=1, replica_groups=mesh['za'=4,'zb'=4,'core'=2,'x'=4,'y'=4] {'x','y'}, dimensions={0} | all-to-all | bytes 4849664 | tf_op jit(solution)/shard_map/all_to_all | solution.py:227
  112.4 2.9 %arrive_kernel.1 = (f32[4,72,128]{2,1,0:T(8,128)}, f32[80,128]{1,0:T(8,128)}) custom-call(s32[32]{0:T(128)} %sections.7, f32[16,296,128]{2,1,0:T(8,128)} %all_to_all.27.got, bf16[4,128,128]{2,1,0:T(8,128)(2,1)} %backward.3), custom_call_target="tpu_custom_call" | custom-call | tf_op jit(solution)/shard_map/arrive_kernel/pallas_call | solution.py:213
  115.3 6.5 %collective-permute-start.1 = (f32[80,128]{1,0:T(8,128)}, f32[80,128]{1,0:T(8,128)S(1)}, u32[]{:S(2)}, u32[]{:S(2)}) collective-permute-start(f32[80,128]{1,0:T(8,128)} %get-tuple-element.18.own), channel_id=1, source_target_pairs={{0,16},{16,0},{1,17},{17,1},{2,18},{18,2},{3,19},{19,3},{4,20},{20... | collective-permute-start | bytes 122888 | tf_op jit(solution)/shard_map/ppermute | solution.py:223
  121.8 1.1 collective-permute-done.1.other
  122.9 0.0 copy-start.1
  122.9 0.6 copy-done.1
  123.5 1.9 %back_pair_kernel.1 = f32[4,80,128]{2,1,0:T(8,128)} custom-call(f32[80,128]{1,0:T(8,128)} %get-tuple-element.18.own, f32[80,128]{1,0:T(8,128)} %copy-done.1, f32[320,128]{1,0:T(8,128)} %get-tuple-element.14.own.chunk, f32[320,128]{1,0:T(8,128)} %copy-done), custom_call_target="tpu_custom_call" | custom-call | tf_op jit(solution)/shard_map/back_pair_kernel/pallas_call | solution.py:213
  125.4 10.8 %all_to_all.28.got = f32[4,80,128]{2,1,0:T(8,128)} all-to-all(f32[4,80,128]{2,1,0:T(8,128)} %back_pair_kernel.1), channel_id=1, replica_groups=mesh['za'=4,'zb'=4,'core'=2,'x'=4,'y'=4] {'zb'}, dimensions={0} | all-to-all | bytes 327680 | tf_op jit(solution)/shard_map/all_to_all | solution.py:227
  136.2 2.3 %back_group_kernel.1 = (f32[4,80,128]{2,1,0:T(8,128)}, f32[72,128]{1,0:T(8,128)}) custom-call(f32[4,80,128]{2,1,0:T(8,128)} %all_to_all.28.got, f32[4,320,128]{2,1,0:T(8,128)} %all_to_all.25.got.maps), custom_call_target="tpu_custom_call" | custom-call | tf_op jit(solution)/shard_map/back_group_kernel/pallas_call | solution.py:213
  138.5 19.6 %all_to_all.29.got = f32[4,80,128]{2,1,0:T(8,128)} all-to-all(f32[4,80,128]{2,1,0:T(8,128)} %get-tuple-element.19), channel_id=1, replica_groups=mesh['za'=4,'zb'=4,'core'=2,'x'=4,'y'=4] {'za'}, dimensions={0} | all-to-all | bytes 327680 | tf_op jit(solution)/shard_map/all_to_all | solution.py:227
  158.1 3.3 %final_kernel.1 = (f32[4,64,128]{2,1,0:T(8,128)}, f32[8,64]{1,0:T(8,128)}) custom-call(s32[32]{0:T(128)} %sections.7, f32[4,80,128]{2,1,0:T(8,128)} %all_to_all.29.got, f32[4,192,128]{2,1,0:T(8,128)} %all_to_all.26.got.totals, f32[72,128]{1,0:T(8,128)} %get-tuple-element.20.after, f32[128,128]{1,0:T(8,128)} %get-tuple-element.21.after_map, ...), custom_call_target="tpu_custom_call" | custom-call | tf_op jit(solution)/shard_map/final_kernel/pallas_call | solution.py:213
Async XLA Ops:
  4.7 10.0 %collective-permute-start = (f32[320,128]{1,0:T(8,128)}, f32[320,128]{1,0:T(8,128)S(1)}, u32[]{:S(2)}, u32[]{:S(2)}) collective-permute-start(f32[320,128]{1,0:T(8,128)} %get-tuple-element.14.own.chunk), channel_id=1, source_target_pairs={{0,16},{16,0},{1,17},{17,1},{2,18},{18,2},{3,19},{19,3},{4,20},{20... | collective-permute-start | bytes 491528 | tf_op jit(solution)/shard_map/ppermute | solution.py:223
  14.7 0.7 copy-start
  115.3 7.6 %collective-permute-start.1 = (f32[80,128]{1,0:T(8,128)}, f32[80,128]{1,0:T(8,128)S(1)}, u32[]{:S(2)}, u32[]{:S(2)}) collective-permute-start(f32[80,128]{1,0:T(8,128)} %get-tuple-element.18.own), channel_id=1, source_target_pairs={{0,16},{16,0},{1,17},{17,1},{2,18},{18,2},{3,19},{19,3},{4,20},{20... | collective-permute-start | bytes 122888 | tf_op jit(solution)/shard_map/ppermute | solution.py:223
  122.9 0.6 copy-start.1

commit v2 on v1

--- a/solution.py
+++ b/solution.py
@@ -215,6 +215,7 @@
         out_shape=shapes,
         in_specs=specs,
         out_specs=[VMEM] * len(shapes),
+        compiler_params=pltpu.CompilerParams(vmem_limit_bytes=16 << 20),
         name=kernel.__name__,
     )(*args)
 

time: 165 us -> 149 us (0.903)
  Pallas kernels: 24.3 us -> 9.46 us
  local copies, waits for them, and re-layouts: 1.27 us -> 5.31 us
  blocking collectives: 118 us -> 114 us
    pallas_call x8, Pallas kernels: 24.3 us -> 9.46 us  [call(): pl.pallas_call(kernel, out_shape=shapes, in_specs=specs, out_specs=[VMEM]...]
    unnamed x4 -> x22, local copies, waits for them, and re-layouts: 1.27 us -> 5.31 us
    all_to_all x5, blocking collectives: 118 us -> 114 us  [exchange(): return lax.all_to_all(a, axis, 0, 0, tiled=True)]
where the time goes in v2:
time: 149 us; the launch traced here: 147 us
  blocking collectives  114 us (77%)
  starting transfers between devices  15.5 us (10%)
  Pallas kernels  9.46 us (6%)
  local copies, waits for them, and re-layouts  5.31 us (4%)
  waiting for transfers between devices  1.85 us (1%)
    all_to_all x5, blocking collectives, exchange(): return lax.all_to_all(a, axis, 0, 0, tiled=True)  114 us
    ppermute x2, starting transfers between devices, swap(): return lax.ppermute(a, 'core', [(0, 1), (1, 0)])  15.5 us
    pallas_call x8, Pallas kernels, call(): pl.pallas_call(kernel, out_shape=shapes, in_specs=specs, out_specs=[VMEM]...  9.46 us
    unnamed x22, local copies, waits for them, and re-layouts  5.31 us
  transfers between devices with their start and end apart: 2, of which 2 were waited for; matrix products, arithmetic and copies ran while one was open for 0% of the time, Pallas kernels for 0%

profile of v2, /device:TPU:1, one launch (start us, length us, event | category | flops | bytes accessed | tf_op | source)
XLA Modules:
  0.0 146.5 jit_solution(15324535210678650186)
XLA Ops:
  0.6 0.0 copy-start
  0.6 1.6 %copy-done = bf16[4,128,2048]{2,1,0:T(8,128)(2,1)S(1)} copy-done((bf16[4,128,2048]{2,1,0:T(8,128)(2,1)S(1)}, bf16[4,128,2048]{2,1,0:T(8,128)(2,1)}, u32[]{:S(2)}) %copy-start) | copy-done | bytes 2097176
  2.2 0.0 copy-start.2
  2.2 1.2 copy-done.2
  3.4 0.0 copy-start.3
  3.5 0.9 copy-done.3
  4.4 0.0 copy-start.5
  4.4 0.9 copy-done.5
  5.3 0.0 copy-start.7
  5.3 0.7 copy-done.7
  5.9 1.9 %local_kernel.1 = (f32[4,192,128]{2,1,0:T(8,128)S(1)}, f32[4,128,128]{2,1,0:T(8,128)S(1)}, f32[320,128]{1,0:T(8,128)S(1)}) custom-call(s32[32]{0:T(128)S(1)} %copy-done.7, bf16[4,64,2048]{2,1,0:T(8,128)(2,1)S(1)} %copy-done.2, bf16[4,128,2048]{2,1,0:T(8,128)(2,1)S(1)} %copy-done, bf16[4,128,128]{2,1,0:T(8,128)(2,1)S(1)} %copy-done.5, ...), custom_call_target="tpu_custom_call" | custom-call | tf_op jit(solution)/shard_map/local_kernel/pallas_call | solution.py:213
  7.9 0.0 copy-start.1
  7.9 0.0 copy-start.6
  7.9 0.0 copy-start.8
  7.9 8.9 %collective-permute-start = (f32[320,128]{1,0:T(8,128)S(1)}, f32[320,128]{1,0:T(8,128)S(1)}, u32[]{:S(2)}, u32[]{:S(2)}) collective-permute-start(f32[320,128]{1,0:T(8,128)S(1)} %get-tuple-element.14.own.chunk), channel_id=1, source_target_pairs={{0,16},{16,0},{1,17},{17,1},{2,18},{18,2},{3,19},{19,3},{4,20},{20... | collective-permute-start | bytes 491528 | tf_op jit(solution)/shard_map/ppermute | solution.py:224
  16.8 1.0 collective-permute-done.other.other_chunk
  17.8 0.2 pair_kernel.1
  18.0 19.4 %all_to_all.25.got.maps = f32[4,320,128]{2,1,0:T(8,128)S(1)} all-to-all(f32[4,320,128]{2,1,0:T(8,128)S(1)} %pair_kernel.1), channel_id=1, replica_groups=mesh['za'=4,'zb'=4,'core'=2,'x'=4,'y'=4] {'zb'}, dimensions={0} | all-to-all | bytes 1310720 | tf_op jit(solution)/shard_map/all_to_all | solution.py:228
  37.5 0.7 group_kernel.1
  38.2 30.9 %all_to_all.26.got.totals = f32[4,192,128]{2,1,0:T(8,128)S(1)} all-to-all(f32[4,192,128]{2,1,0:T(8,128)S(1)} %get-tuple-element.15), channel_id=1, replica_groups=mesh['za'=4,'zb'=4,'core'=2,'x'=4,'y'=4] {'za'}, dimensions={0} | all-to-all | bytes 786432 | tf_op jit(solution)/shard_map/all_to_all | solution.py:228
  69.1 0.0 copy-done.1
  69.1 0.0 copy-done.6
  69.1 0.0 copy-done.8
  69.1 2.4 %source_kernel.1 = f32[16,296,128]{2,1,0:T(8,128)S(1)} custom-call(s32[32]{0:T(128)S(1)} %copy-done.8, f32[4,192,128]{2,1,0:T(8,128)S(1)} %all_to_all.26.got.totals, f32[192,128]{1,0:T(8,128)S(1)} %get-tuple-element.16.before, f32[320,128]{1,0:T(8,128)S(1)} %collective-permute-done.other.other_chunk, f32[4,192,128]{2,1,0:T(8,128)S(1)} %get-tuple-element.17.states, ...), custom_call_target="tpu_custom_call" | custom-call | tf_op jit(solution)/shard_map/source_kernel/pallas_call | solution.py:213
  71.5 0.0 copy-start.4
  71.5 34.6 %all_to_all.27.got = f32[16,296,128]{2,1,0:T(8,128)S(1)} all-to-all(f32[16,296,128]{2,1,0:T(8,128)S(1)} %source_kernel.1), channel_id=1, replica_groups=mesh['za'=4,'zb'=4,'core'=2,'x'=4,'y'=4] {'x','y'}, dimensions={0} | all-to-all | bytes 4849664 | tf_op jit(solution)/shard_map/all_to_all | solution.py:228
  106.1 0.0 copy-done.4
  106.1 0.0 copy-start.9
  106.1 0.0 copy-start.10
  106.1 1.1 arrive_kernel.1
  107.2 6.6 %collective-permute-start.1 = (f32[80,128]{1,0:T(8,128)S(1)}, f32[80,128]{1,0:T(8,128)S(1)}, u32[]{:S(2)}, u32[]{:S(2)}) collective-permute-start(f32[80,128]{1,0:T(8,128)S(1)} %get-tuple-element.18.own), channel_id=1, source_target_pairs={{0,16},{16,0},{1,17},{17,1},{2,18},{18,2},{3,19},{19,3},{4,20},{20... | collective-permute-start | bytes 122888 | tf_op jit(solution)/shard_map/ppermute | solution.py:224
  113.8 0.8 collective-permute-done.1.other
  114.6 0.2 back_pair_kernel.1
  114.8 9.1 %all_to_all.28.got = f32[4,80,128]{2,1,0:T(8,128)S(1)} all-to-all(f32[4,80,128]{2,1,0:T(8,128)S(1)} %back_pair_kernel.1), channel_id=1, replica_groups=mesh['za'=4,'zb'=4,'core'=2,'x'=4,'y'=4] {'zb'}, dimensions={0} | all-to-all | bytes 327680 | tf_op jit(solution)/shard_map/all_to_all | solution.py:228
  123.9 0.4 back_group_kernel.1
  124.3 19.8 %all_to_all.29.got = f32[4,80,128]{2,1,0:T(8,128)S(1)} all-to-all(f32[4,80,128]{2,1,0:T(8,128)S(1)} %get-tuple-element.19), channel_id=1, replica_groups=mesh['za'=4,'zb'=4,'core'=2,'x'=4,'y'=4] {'za'}, dimensions={0} | all-to-all | bytes 327680 | tf_op jit(solution)/shard_map/all_to_all | solution.py:228
  144.0 0.0 copy-done.9
  144.0 0.0 copy-done.10
  144.0 2.5 %final_kernel.1 = (f32[4,64,128]{2,1,0:T(8,128)}, f32[8,64]{1,0:T(8,128)}) custom-call(s32[32]{0:T(128)S(1)} %copy-done.8, f32[4,80,128]{2,1,0:T(8,128)S(1)} %all_to_all.29.got, f32[4,192,128]{2,1,0:T(8,128)S(1)} %all_to_all.26.got.totals, f32[72,128]{1,0:T(8,128)S(1)} %get-tuple-element.20.after, f32[128,128]{1,0:T(8,128)S(1)} %get-tuple-element.21.after_map, ...), custom_call_target="tpu_custom_call" | custom-call | tf_op jit(solution)/shard_map/final_kernel/pallas_call | solution.py:213
Async XLA Ops:
  0.6 1.6 %copy-start = (bf16[4,128,2048]{2,1,0:T(8,128)(2,1)S(1)}, bf16[4,128,2048]{2,1,0:T(8,128)(2,1)}, u32[]{:S(2)}) copy-start(bf16[4,128,2048]{2,1,0:T(8,128)(2,1)} %inverse.3) | copy-start | bytes 6291460
  2.2 1.2 copy-start.2
  3.4 0.9 copy-start.3
  4.4 0.9 copy-start.5
  5.3 0.7 copy-start.7
  7.9 61.2 %copy-start.1 = (bf16[4,128,2048]{2,1,0:T(8,128)(2,1)S(1)}, bf16[4,128,2048]{2,1,0:T(8,128)(2,1)}, u32[]{:S(2)}) copy-start(bf16[4,128,2048]{2,1,0:T(8,128)(2,1)} %inverse.3) | copy-start | bytes 6291460
  7.9 61.2 %copy-start.6 = (bf16[4,8,128]{2,1,0:T(8,128)(2,1)S(1)}, bf16[4,8,128]{2,1,0:T(8,128)(2,1)}, u32[]{:S(2)}) copy-start(bf16[4,8,128]{2,1,0:T(8,128)(2,1)} %arrow.1) | copy-start | bytes 24580
  7.9 61.2 %copy-start.8 = (s32[32]{0:T(128)S(1)}, s32[32]{0:T(128)}, u32[]{:S(2)}) copy-start(s32[32]{0:T(128)} %sections.7) | copy-start | bytes 388
  7.9 9.9 %collective-permute-start = (f32[320,128]{1,0:T(8,128)S(1)}, f32[320,128]{1,0:T(8,128)S(1)}, u32[]{:S(2)}, u32[]{:S(2)}) collective-permute-start(f32[320,128]{1,0:T(8,128)S(1)} %get-tuple-element.14.own.chunk), channel_id=1, source_target_pairs={{0,16},{16,0},{1,17},{17,1},{2,18},{18,2},{3,19},{19,3},{4,20},{20... | collective-permute-start | bytes 491528 | tf_op jit(solution)/shard_map/ppermute | solution.py:224
  71.5 34.6 %copy-start.4 = (bf16[4,128,128]{2,1,0:T(8,128)(2,1)S(1)}, bf16[4,128,128]{2,1,0:T(8,128)(2,1)}, u32[]{:S(2)}) copy-start(bf16[4,128,128]{2,1,0:T(8,128)(2,1)} %backward.3) | copy-start | bytes 393220
  106.1 37.9 %copy-start.9 = (f32[64,8]{0,1:T(8,128)S(1)}, f32[64,8]{0,1:T(8,128)}, u32[]{:S(2)}) copy-start(f32[64,8]{0,1:T(8,128)} %param.10) | copy-start | bytes 6148
  106.1 37.9 %copy-start.10 = (f32[8,8]{1,0:T(8,128)S(1)}, f32[8,8]{1,0:T(8,128)}, u32[]{:S(2)}) copy-start(f32[8,8]{1,0:T(8,128)} %tip_inverse.1) | copy-start | bytes 772
  107.2 7.4 %collective-permute-start.1 = (f32[80,128]{1,0:T(8,128)S(1)}, f32[80,128]{1,0:T(8,128)S(1)}, u32[]{:S(2)}, u32[]{:S(2)}) collective-permute-start(f32[80,128]{1,0:T(8,128)S(1)} %get-tuple-element.18.own), channel_id=1, source_target_pairs={{0,16},{16,0},{1,17},{17,1},{2,18},{18,2},{3,19},{19,3},{4,20},{20... | collective-permute-start | bytes 122888 | tf_op jit(solution)/shard_map/ppermute | solution.py:224

commit v3 on v2

v3 whole, which is shorter than its diff:
```python
import jax
import jax.numpy as jnp
from jax import lax
from jax.experimental import pallas as pl
from jax.experimental.pallas import tpu as pltpu
from jax.sharding import Mesh
from jax.sharding import PartitionSpec as P

F32 = jnp.float32
BF16 = jnp.bfloat16
TM = ("zg", "zp", "core")
SPACE = ("x", "y")
NEAR = ("zp", "core")
FAR = ("zg", "core")
T = 4
R = 64
F = 8
W = 128
N = 16
G = R + F
L = 4
Q = 8
HI = lax.Precision.HIGHEST


def split(x):
    high = x.astype(BF16)
    return high, (x - high.astype(F32)).astype(BF16)


def dot(a, b, dims):
    return lax.dot_general(a, b, ((dims[:1], dims[1:]), ((), ())), preferred_element_type=F32)


def times(x, m):
    xh, xl = split(x)
    mh, ml = split(m)
    return dot(jnp.concatenate([xh, xl, xh], 1), jnp.concatenate([mh, mh, ml], 0), (1, 0))


def times_t(x, c):
    xh, xl = split(x)
    return dot(jnp.concatenate([xh, xl], 1), jnp.concatenate([c, c], 1), (1, 1))


def eye(dtype):
    rows = lax.broadcasted_iota(jnp.int32, (W, W), 0)
    cols = lax.broadcasted_iota(jnp.int32, (W, W), 1)
    return jnp.where(rows == cols, 1.0, 0.0).astype(dtype)


def near_index():
    return lax.axis_index("zp") * 2 + lax.axis_index("core")


def live_count(sections):
    return sections[lax.axis_index("zg") * L + near_index()]


def join(first, then):
    out = times(first, then[R : R + W])
    return jnp.concatenate([out[:R] + then[:R], out[R:]], 0)


def half_of(x):
    rows = x.shape[0] // 2
    return jnp.where(lax.axis_index("core") == 0, x[:rows], x[rows:])


def local_kernel(
    sections_in, side_in, inverse_in, forward_in, states, chunk, sections, side, inverse, forward, sems
):
    copies = [
        pltpu.make_async_copy(sections_in, sections, sems.at[0]),
        pltpu.make_async_copy(forward_in, forward, sems.at[1]),
    ]
    for t in range(T):
        copies.append(pltpu.make_async_copy(side_in.at[t], side.at[t], sems.at[2 + 2 * t]))
        copies.append(pltpu.make_async_copy(inverse_in.at[t], inverse.at[t], sems.at[3 + 2 * t]))
    for copy in copies:
        copy.start()
    copies[0].wait()
    copies[1].wait()
    live = live_count(sections)
    state = None
    for t in range(T):
        copies[2 + 2 * t].wait()
        copies[3 + 2 * t].wait()
        driven = dot(side[t], inverse[t], (1, 1))
        if t == 0:
            state = jnp.concatenate([driven, -dot(eye(BF16), forward[0], (1, 1))], 0)
        else:
            moved = times_t(state, forward[t])
            state = jnp.where(
                t < live, jnp.concatenate([driven - moved[:R], -moved[R:]], 0), state
            )
        states[t] = state
    chunk[...] = state


def group_kernel(got, out, before):
    me = near_index()
    total = got[0]
    before[...] = jnp.concatenate([jnp.zeros((R, W), F32), eye(F32)], 0)
    for j in range(1, L):
        before[...] = jnp.where(me == j, total, before[...])
        total = join(total, got[j])
    out[...] = half_of(total)


def source_kernel(sections, got, before, states, inverse, arrow, out):
    group = lax.axis_index("zg")
    live = live_count(sections)
    entry = jnp.where(group > 0, got[0, :R], 0.0)
    for j in range(1, Q - 1):
        mapping = jnp.concatenate([got[2 * j, R:], got[2 * j + 1]], 0)
        entry = jnp.where(j < group, times(entry, mapping) + got[2 * j, :R], entry)
    entry = times(entry, before[R:]) + before[:R]
    total = jnp.zeros((F, W), F32)
    pad = jnp.zeros((W - R, W), BF16)
    for t in range(T):
        state = states[t]
        state = jnp.where(t < live, state[:R] + times(entry, state[R:]), 0.0)
        high, low = split(state)
        total += dot(arrow[t], jnp.concatenate([high, pad], 0), (1, 1))
        rows = jnp.concatenate([high, low, arrow[t], jnp.zeros((F, W), BF16)], 0)
        terms = dot(rows, inverse[t], (1, 0))
        for n in range(N):
            cols = slice(n * W, (n + 1) * W)
            out[n, t * G : t * G + R] = terms[:R, cols] + terms[R : 2 * R, cols]
            out[n, t * G + R : (t + 1) * G] = terms[2 * R : 2 * R + F, cols]
    for n in range(N):
        out[n, T * G :] = total


def maps_kernel(sections, backward, maps, chunk):
    live = live_count(sections)
    mapping = eye(F32)
    for t in reversed(range(T)):
        mapping = jnp.where(t < live, -times_t(mapping, backward[t]), mapping)
        maps[t] = mapping
    chunk[...] = mapping


def group_maps_kernel(got, out, after):
    me = near_index()
    total = got[L - 1]
    after[...] = eye(F32)
    for j in reversed(range(L - 1)):
        after[...] = jnp.where(me == j, total, after[...])
        total = times(total, got[j])
    out[...] = half_of(total)


def arrive_kernel(sections, got, backward, sums, chunk):
    live = live_count(sections)
    whole = got[0]
    for n in range(1, N):
        whole = whole + got[n]
    state = jnp.zeros((G, W), F32)
    for t in reversed(range(T)):
        source = whole[t * G : (t + 1) * G]
        state = jnp.where(t < live, source - times_t(state, backward[t]), state)
        sums[t] = state
    chunk[:G] = state
    chunk[G:] = whole[T * G :]


def back_group_kernel(got, maps, out, after):
    me = near_index()
    total = got[L - 1, :G]
    after[...] = jnp.zeros((G, W), F32)
    for j in reversed(range(L - 1)):
        after[...] = jnp.where(me == j, total, after[...])
        total = times(total, maps[j]) + got[j, :G]
    whole = ((got[0, G:] + got[1, G:]) + got[2, G:]) + got[3, G:]
    out[...] = half_of(jnp.concatenate([total, whole], 0))


def final_kernel(
    sections, got, totals, after, after_map, sums, maps, side, tip_inverse, out, tip_out
):
    group = lax.axis_index("zg")
    live = live_count(sections)
    edge = (G + F) // 2
    whole = got[1, edge - F :]
    for j in range(1, Q):
        whole = whole + got[2 * j + 1, edge - F :]
    gap = side[...] - whole[:, :R]
    tip = lax.dot_general(
        tip_inverse[...], gap, (((1,), (0,)), ((), ())), precision=HI, preferred_element_type=F32
    )
    tip = lax.dot_general(
        tip_inverse[...], tip, (((0,), (0,)), ((), ())), precision=HI, preferred_element_type=F32
    )
    tip_out[...] = tip

    def offset(j):
        return jnp.concatenate([got[2 * j], got[2 * j + 1, : edge - F]], 0)

    entry = jnp.where(group < Q - 1, offset(Q - 1), 0.0)
    for j in reversed(range(1, Q - 1)):
        mapping = jnp.concatenate([totals[2 * j], totals[2 * j + 1]], 0)
        entry = jnp.where(j > group, times(entry, mapping) + offset(j), entry)
    entry = times(entry, after_map[...]) + after[...]
    tip_high, tip_low = split(tip)
    weights = jnp.concatenate(
        [tip_high.astype(F32), tip_low.astype(F32), tip_high.astype(F32)], 0
    ).astype(BF16)
    for t in range(T):
        state = sums[t] + times(entry, maps[t])
        high, low = split(state[R:])
        parts = jnp.concatenate([high.astype(F32), high.astype(F32), low.astype(F32)], 0).astype(BF16)
        out[t] = jnp.where(t < live, state[:R] - dot(weights, parts, (0, 0)), 0.0)


VMEM = pl.BlockSpec(memory_space=pltpu.VMEM)
SMEM = pl.BlockSpec(memory_space=pltpu.SMEM)
HBM = pl.BlockSpec(memory_space=pltpu.HBM)


def call(kernel, shapes, *args, own_copies=False, scratch=()):
    specs = [HBM if own_copies else SMEM if a.dtype == jnp.int32 else VMEM for a in args]
    shapes = [jax.ShapeDtypeStruct(s, F32) for s in shapes]
    return pl.pallas_call(
        kernel,
        out_shape=shapes,
        in_specs=specs,
        out_specs=[VMEM] * len(shapes),
        scratch_shapes=scratch,
        compiler_params=pltpu.CompilerParams(vmem_limit_bytes=16 << 20),
    )(*args)


def on_device(
    sections, right_side, tip_side, diag_inverse, forward_coupling, backward_coupling, arrow_rows, tip_inverse
):
    states, chunk = call(
        local_kernel,
        [(T, R + W, W), (R + W, W)],
        sections,
        right_side,
        diag_inverse,
        forward_coupling,
        own_copies=True,
        scratch=(
            pltpu.SMEM(sections.shape, jnp.int32),
            pltpu.VMEM(right_side.shape, BF16),
            pltpu.VMEM(diag_inverse.shape, BF16),
            pltpu.VMEM(forward_coupling.shape, BF16),
            pltpu.SemaphoreType.DMA((2 + 2 * T,)),
        ),
    )
    got = lax.all_gather(chunk, NEAR)
    out, before = call(group_kernel, [((R + W) // 2, W), (R + W, W)], got)
    got = lax.all_gather(out, FAR)
    (out,) = call(
        source_kernel,
        [(N, T * G + F, W)],
        sections,
        got,
        before,
        states,
        diag_inverse,
        arrow_rows,
    )
    got = lax.all_to_all(out, SPACE, 0, 0, tiled=True)
    maps, chunk = call(maps_kernel, [(T, W, W), (W, W)], sections, backward_coupling)
    near_maps = lax.all_gather(chunk, NEAR)
    out, after_map = call(group_maps_kernel, [(W // 2, W), (W, W)], near_maps)
    far_maps = lax.all_gather(out, FAR)
    sums, chunk = call(arrive_kernel, [(T, G, W), (G + F, W)], sections, got, backward_coupling)
    got = lax.all_gather(chunk, NEAR)
    out, after = call(back_group_kernel, [((G + F) // 2, W), (G, W)], got, near_maps)
    got = lax.all_gather(out, FAR)
    solved, tip = call(
        final_kernel,
        [(T, R, W), (F, R)],
        sections,
        got,
        far_maps,
        after,
        after_map,
        sums,
        maps,
        tip_side.T,
        tip_inverse,
    )
    return solved, tip.T


def solution(mesh):
    torus = Mesh(mesh.devices.reshape(Q, 2, 2, 4, 4), TM + SPACE)
    return jax.shard_map(
        on_device,
        mesh=torus,
        in_specs=(
            P(),
            P(TM, None, None),
            P(),
            P(TM, SPACE, None),
            P(TM, SPACE, None),
            P(TM, SPACE, None),
            P(TM, None, SPACE),
            P(),
        ),
        out_specs=(P(TM, None, SPACE), P()),
        check_vma=False,
    )
```

time: 149 us -> 119 us (0.80); the launches traced: 147 us -> 119 us
  blocking collectives: 114 us -> 87.6 us
  starting transfers between devices: 15.5 us -> 6.88 us
  waiting for transfers between devices: 1.85 us -> 6.03 us
  Pallas kernels: 9.46 us -> 11.5 us
    all_to_all x5 -> x0, blocking collectives: 114 us -> none  [exchange(): return lax.all_to_all(a, axis, 0, 0, tiled=True)]
    all_gather x0 -> x6, blocking collectives: none -> 87.6 us  [the longest x2 42.4 us: on_device(): got = lax.all_gather(out, FAR)]
    ppermute x2 -> x0, starting transfers between devices: 15.5 us -> none  [swap(): return lax.ppermute(a, 'core', [(0, 1), (1, 0)])]
    all_to_all x0 -> x1, starting transfers between devices: none -> 6.88 us  [on_device(): got = lax.all_to_all(out, SPACE, 0, 0, tiled=True)]
    all_to_all x0 -> x1, waiting for transfers between devices: none -> 6.03 us  [on_device(): got = lax.all_to_all(out, SPACE, 0, 0, tiled=True)]
    pallas_call x8, Pallas kernels: 9.46 us -> 11.5 us  [call(): pl.pallas_call(kernel, out_shape=shapes, in_specs=specs, out_specs=[VMEM]...]
    ppermute x2 -> x0, waiting for transfers between devices: 1.85 us -> none  [swap(): return lax.ppermute(a, 'core', [(0, 1), (1, 0)])]
    unnamed x22 -> x26, local copies, waits for them, and re-layouts: 5.31 us -> 5.85 us
  transfers between devices with their start and end apart: 2 -> 1, of which waited for: 2 -> 1; matrix products, arithmetic and copies ran while one was open for 0% -> 0% of each run, Pallas kernels for 0% -> 1%
where the time goes in v3:
time: 119 us
  blocking collectives  87.6 us (74%)
  Pallas kernels  11.5 us (10%)
  starting transfers between devices  6.88 us (6%)
  waiting for transfers between devices  6.03 us (5%)
  local copies, waits for them, and re-layouts  5.85 us (5%)
    all_gather x2, blocking collectives, on_device(): got = lax.all_gather(out, FAR)  42.4 us
    all_gather x2, blocking collectives, on_device(): got = lax.all_gather(chunk, NEAR)  20.2 us
    all_gather x1, blocking collectives, on_device(): far_maps = lax.all_gather(out, FAR)  19 us
    pallas_call x8, Pallas kernels, call(): pl.pallas_call(kernel, out_shape=shapes, in_specs=specs, out_specs=[VMEM]...  11.5 us
    all_to_all x1, starting transfers between devices, on_device(): got = lax.all_to_all(out, SPACE, 0, 0, tiled=True)  6.88 us
    all_gather x1, blocking collectives, on_device(): near_maps = lax.all_gather(chunk, NEAR)  6.05 us
    all_to_all x1, waiting for transfers between devices, on_device(): got = lax.all_to_all(out, SPACE, 0, 0, tiled=True)  6.03 us
    unnamed x26, local copies, waits for them, and re-layouts  5.85 us
  transfers between devices with their start and end apart: 1, of which 1 were waited for; matrix products, arithmetic and copies ran while one was open for 0% of the time, Pallas kernels for 1%

profile of v3, /device:TPU:1, one launch (start us, length us, event | category | flops | bytes accessed | tf_op | source)
XLA Modules:
  0.0 118.6 jit_solution(12343932719470733603)
XLA Ops:
  0.6 0.0 copy-start.1
  0.6 1.6 %copy-done.1 = bf16[4,128,2048]{2,1,0:T(8,128)(2,1)S(1)} copy-done((bf16[4,128,2048]{2,1,0:T(8,128)(2,1)S(1)}, bf16[4,128,2048]{2,1,0:T(8,128)(2,1)}, u32[]{:S(2)}) %copy-start.1) | copy-done | bytes 2097176
  2.2 0.0 copy-start.3
  2.2 1.2 %copy-done.3 = bf16[4,64,2048]{2,1,0:T(8,128)(2,1)S(1)} copy-done((bf16[4,64,2048]{2,1,0:T(8,128)(2,1)S(1)}, bf16[4,64,2048]{2,1,0:T(8,128)(2,1)}, u32[]{:S(2)}) %copy-start.3) | copy-done | bytes 1048600
  3.4 0.0 copy-start.7
  3.5 0.9 copy-done.7
  4.4 0.0 copy-start.8
  4.4 0.7 copy-done.8
  5.0 0.0 copy-start.2
  5.0 0.0 copy-start.10
  5.0 2.3 %shard_map.95 = (f32[4,192,128]{2,1,0:T(8,128)S(1)}, f32[192,128]{1,0:T(8,128)S(1)}) custom-call(s32[32]{0:T(128)S(1)} %copy-done.8, bf16[4,64,2048]{2,1,0:T(8,128)(2,1)S(1)} %copy-done.3, bf16[4,128,2048]{2,1,0:T(8,128)(2,1)S(1)} %copy-done.1, bf16[4,128,128]{2,1,0:T(8,128)(2,1)S(1)} %copy-done.7), custom_call_target="tpu_custom_call" | custom-call | tf_op jit(solution)/shard_map/pallas_call | solution.py:225
  7.4 12.8 %all-gather = f32[768,128]{1,0:T(8,128)S(1)} all-gather(f32[192,128]{1,0:T(8,128)S(1)} %get-tuple-element.16), channel_id=2, replica_groups=mesh['zg'=8,'zp'=2,'core'=2,'x'=4,'y'=4] {'zp','core'}, dimensions={0}, use_global_device_ids=true | all-gather | bytes 491520 | tf_op jit(solution)/shard_map/all_gather | solution.py:254
  20.2 0.5 shard_map.96
  20.6 24.2 %all-gather.1 = f32[1536,128]{1,0:T(8,128)S(1)} all-gather(f32[96,128]{1,0:T(8,128)S(1)} %get-tuple-element.17), channel_id=3, replica_groups=mesh['zg'=8,'zp'=2,'core'=2,'x'=4,'y'=4] {'zg','core'}, dimensions={0}, use_global_device_ids=true | all-gather | bytes 835584 | tf_op jit(solution)/shard_map/all_gather | solution.py:256
  44.9 0.0 copy-done.2
  44.9 0.0 copy-done.10
  44.9 2.8 %shard_map.97 = f32[16,296,128]{2,1,0:T(8,128)S(1)} custom-call(s32[32]{0:T(128)S(1)} %copy-done.8, f32[16,96,128]{2,1,0:T(8,128)S(1)} %bitcast.8, f32[192,128]{1,0:T(8,128)S(1)} %get-tuple-element.18.before, f32[4,192,128]{2,1,0:T(8,128)S(1)} %get-tuple-element.19.states, bf16[4,128,2048]{2,1,0:T(8,128)(2,1)S(1)} %copy-done.2, bf16[4,8,128]{2,1,0:T(8,128)(2,1)S(1)} %copy-done.10), custom_call_target="tpu_custom_call" | custom-call | tf_op jit(solution)/shard_map/pallas_call | solution.py:225
  47.6 0.0 copy-start
  47.7 1.4 %copy-done = f32[16,296,128]{2,1,0:T(8,128)} copy-done((f32[16,296,128]{2,1,0:T(8,128)}, f32[16,296,128]{2,1,0:T(8,128)S(1)}, u32[]{:S(2)}) %copy-start) | copy-done | bytes 2424856
  49.1 0.0 copy-start.4
  49.1 0.0 copy-start.9
  49.1 6.9 %all-to-all-start = ((f32[16,296,128]{2,1,0:T(8,128)}), f32[16,296,128]{2,1,0:T(8,128)S(1)}, u32[]{:S(2)}, u32[]{:S(2)}) async-start(f32[16,296,128]{2,1,0:T(8,128)} %copy-done), calls=%async_computation | async-start | bytes 4849664 | tf_op jit(solution)/shard_map/all_to_all | solution.py:267
  56.0 0.0 copy-done.4
  56.0 0.0 copy-done.9
  56.0 0.0 copy-start.11
  56.0 0.0 copy-start.12
  56.0 1.1 shard_map.99
  57.1 0.0 copy-start.5
  57.1 6.1 %all-gather.3 = f32[512,128]{1,0:T(8,128)S(1)} all-gather(f32[128,128]{1,0:T(8,128)S(1)} %get-tuple-element.21), channel_id=5, replica_groups=mesh['zg'=8,'zp'=2,'core'=2,'x'=4,'y'=4] {'zp','core'}, dimensions={0}, use_global_device_ids=true | all-gather | bytes 327680 | tf_op jit(solution)/shard_map/all_gather | solution.py:269
  63.2 0.4 shard_map.101
  63.6 0.0 copy-done.5
  63.6 19.0 %all-gather.5 = f32[1024,128]{1,0:T(8,128)S(1)} all-gather(f32[64,128]{1,0:T(8,128)S(1)} %get-tuple-element.23), channel_id=7, replica_groups=mesh['zg'=8,'zp'=2,'core'=2,'x'=4,'y'=4] {'zg','core'}, dimensions={0}, use_global_device_ids=true | all-gather | bytes 557056 | tf_op jit(solution)/shard_map/all_gather | solution.py:271
  82.6 6.0 %all-to-all-done.got = f32[16,296,128]{2,1,0:T(8,128)S(1)} async-done(((f32[16,296,128]{2,1,0:T(8,128)}), f32[16,296,128]{2,1,0:T(8,128)S(1)}, u32[]{:S(2)}, u32[]{:S(2)}) %all-to-all-start) | async-done | bytes 2424864 | tf_op jit(solution)/shard_map/all_to_all | solution.py:267
  88.7 0.0 copy-start.6
  88.7 1.1 shard_map.98
  89.7 7.4 %all-gather.2 = f32[320,128]{1,0:T(8,128)S(1)} all-gather(f32[80,128]{1,0:T(8,128)S(1)} %get-tuple-element.20), channel_id=4, replica_groups=mesh['zg'=8,'zp'=2,'core'=2,'x'=4,'y'=4] {'zp','core'}, dimensions={0}, use_global_device_ids=true | all-gather | bytes 204800 | tf_op jit(solution)/shard_map/all_gather | solution.py:273
  97.2 0.4 shard_map.100
  97.6 18.2 %all-gather.4 = f32[640,128]{1,0:T(8,128)S(1)} all-gather(f32[40,128]{1,0:T(8,128)S(1)} %get-tuple-element.22), channel_id=6, replica_groups=mesh['zg'=8,'zp'=2,'core'=2,'x'=4,'y'=4] {'zg','core'}, dimensions={0}, use_global_device_ids=true | all-gather | bytes 348160 | tf_op jit(solution)/shard_map/all_gather | solution.py:275
  115.7 0.0 copy-done.11
  115.7 0.0 copy-done.12
  115.7 0.0 copy-done.6
  115.7 2.9 %shard_map.102 = (f32[4,64,128]{2,1,0:T(8,128)}, f32[8,64]{1,0:T(8,128)}) custom-call(s32[32]{0:T(128)S(1)} %copy-done.9, f32[16,40,128]{2,1,0:T(8,128)S(1)} %bitcast.13, f32[16,64,128]{2,1,0:T(8,128)S(1)} %bitcast.11, f32[72,128]{1,0:T(8,128)S(1)} %get-tuple-element.24.after, f32[128,128]{1,0:T(8,128)S(1)} %get-tuple-element.25.after_map, ...), custom_call_target="tpu_custom_call" | custom-call | tf_op jit(solution)/shard_map/pallas_call | solution.py:225
Async XLA Ops:
  0.6 1.6 %copy-start.1 = (bf16[4,128,2048]{2,1,0:T(8,128)(2,1)S(1)}, bf16[4,128,2048]{2,1,0:T(8,128)(2,1)}, u32[]{:S(2)}) copy-start(bf16[4,128,2048]{2,1,0:T(8,128)(2,1)} %inverse.1) | copy-start | bytes 6291460
  2.2 1.2 %copy-start.3 = (bf16[4,64,2048]{2,1,0:T(8,128)(2,1)S(1)}, bf16[4,64,2048]{2,1,0:T(8,128)(2,1)}, u32[]{:S(2)}) copy-start(bf16[4,64,2048]{2,1,0:T(8,128)(2,1)} %side_in.1) | copy-start | bytes 3145732
  3.4 0.9 copy-start.7
  4.4 0.7 copy-start.8
  5.0 39.8 %copy-start.2 = (bf16[4,128,2048]{2,1,0:T(8,128)(2,1)S(1)}, bf16[4,128,2048]{2,1,0:T(8,128)(2,1)}, u32[]{:S(2)}) copy-start(bf16[4,128,2048]{2,1,0:T(8,128)(2,1)} %inverse.1) | copy-start | bytes 6291460
  5.0 39.8 %copy-start.10 = (bf16[4,8,128]{2,1,0:T(8,128)(2,1)S(1)}, bf16[4,8,128]{2,1,0:T(8,128)(2,1)}, u32[]{:S(2)}) copy-start(bf16[4,8,128]{2,1,0:T(8,128)(2,1)} %arrow.1) | copy-start | bytes 24580
  47.6 1.5 %copy-start = (f32[16,296,128]{2,1,0:T(8,128)}, f32[16,296,128]{2,1,0:T(8,128)S(1)}, u32[]{:S(2)}) copy-start(f32[16,296,128]{2,1,0:T(8,128)S(1)} %shard_map.97) | copy-start | bytes 7274500
  49.1 6.9 %copy-start.4 = (bf16[4,128,128]{2,1,0:T(8,128)(2,1)S(1)}, bf16[4,128,128]{2,1,0:T(8,128)(2,1)}, u32[]{:S(2)}) copy-start(bf16[4,128,128]{2,1,0:T(8,128)(2,1)} %backward.3) | copy-start | bytes 393220
  49.1 6.9 %copy-start.9 = (s32[32]{0:T(128)S(1)}, s32[32]{0:T(128)}, u32[]{:S(2)}) copy-start(s32[32]{0:T(128)} %sections.7) | copy-start | bytes 388
  49.1 39.6 %all-to-all-start = ((f32[16,296,128]{2,1,0:T(8,128)}), f32[16,296,128]{2,1,0:T(8,128)S(1)}, u32[]{:S(2)}, u32[]{:S(2)}) async-start(f32[16,296,128]{2,1,0:T(8,128)} %copy-done), calls=%async_computation | async-start | bytes 4849664 | tf_op jit(solution)/shard_map/all_to_all | solution.py:267
  56.0 59.7 %copy-start.11 = (f32[64,8]{0,1:T(8,128)S(1)}, f32[64,8]{0,1:T(8,128)}, u32[]{:S(2)}) copy-start(f32[64,8]{0,1:T(8,128)} %param.10) | copy-start | bytes 6148
  56.0 59.7 %copy-start.12 = (f32[8,8]{1,0:T(8,128)S(1)}, f32[8,8]{1,0:T(8,128)}, u32[]{:S(2)}) copy-start(f32[8,8]{1,0:T(8,128)} %tip_inverse.1) | copy-start | bytes 772
  57.1 6.5 %copy-start.5 = (f32[4,128,128]{2,1,0:T(8,128)}, f32[4,128,128]{2,1,0:T(8,128)S(1)}, u32[]{:S(2)}) copy-start(f32[4,128,128]{2,1,0:T(8,128)S(1)} %get-tuple-element.27.maps) | copy-start | bytes 786436
  88.7 27.1 %copy-start.6 = (f32[4,128,128]{2,1,0:T(8,128)S(1)}, f32[4,128,128]{2,1,0:T(8,128)}, u32[]{:S(2)}) copy-start(f32[4,128,128]{2,1,0:T(8,128)} %copy-done.5) | copy-start | bytes 786436

commit v4 on v3

--- a/solution.py
+++ b/solution.py
@@ -1,3 +1,5 @@
+import functools
+
 import jax
 import jax.numpy as jnp
 from jax import lax
@@ -20,6 +22,8 @@
 G = R + F
 L = 4
 Q = 8
+EDGE = (G + F) // 2
+GRANT = 66_000_000
 HI = lax.Precision.HIGHEST
 
 
@@ -68,24 +72,43 @@
 
 
 def local_kernel(
-    sections_in, side_in, inverse_in, forward_in, states, chunk, sections, side, inverse, forward, sems
+    sections_in,
+    side_in,
+    inverse_in,
+    forward_in,
+    backward_in,
+    states,
+    maps,
+    chunk,
+    sections,
+    side,
+    inverse,
+    forward,
+    backward,
+    sems,
 ):
     copies = [
         pltpu.make_async_copy(sections_in, sections, sems.at[0]),
-        pltpu.make_async_copy(forward_in, forward, sems.at[1]),
+        pltpu.make_async_copy(backward_in, backward, sems.at[1]),
+        pltpu.make_async_copy(forward_in, forward, sems.at[2]),
     ]
     for t in range(T):
-        copies.append(pltpu.make_async_copy(side_in.at[t], side.at[t], sems.at[2 + 2 * t]))
-        copies.append(pltpu.make_async_copy(inverse_in.at[t], inverse.at[t], sems.at[3 + 2 * t]))
+        copies.append(pltpu.make_async_copy(side_in.at[t], side.at[t], sems.at[3 + 2 * t]))
+        copies.append(pltpu.make_async_copy(inverse_in.at[t], inverse.at[t], sems.at[4 + 2 * t]))
     for copy in copies:
         copy.start()
-    copies[0].wait()
-    copies[1].wait()
+    for copy in copies[:3]:
+        copy.wait()
     live = live_count(sections)
+    mapping = eye(F32)
+    for t in reversed(range(T)):
+        mapping = jnp.where(t < live, -times_t(mapping, backward[t]), mapping)
+        maps[t] = mapping
+    chunk[R + W :] = mapping
     state = None
     for t in range(T):
-        copies[2 + 2 * t].wait()
         copies[3 + 2 * t].wait()
+        copies[4 + 2 * t].wait()
         driven = dot(side[t], inverse[t], (1, 1))
         if t == 0:
             state = jnp.concatenate([driven, -dot(eye(BF16), forward[0], (1, 1))], 0)
@@ -95,17 +118,22 @@
                 t < live, jnp.concatenate([driven - moved[:R], -moved[R:]], 0), state
             )
         states[t] = state
-    chunk[...] = state
-
-
-def group_kernel(got, out, before):
+    chunk[: R + W] = state
+
+
+def group_kernel(got, out, back, before, after):
     me = near_index()
-    total = got[0]
+    total = got[0, : R + W]
     before[...] = jnp.concatenate([jnp.zeros((R, W), F32), eye(F32)], 0)
+    mapping = got[L - 1, R + W :]
+    after[...] = eye(F32)
     for j in range(1, L):
         before[...] = jnp.where(me == j, total, before[...])
-        total = join(total, got[j])
+        total = join(total, got[j, : R + W])
+        after[...] = jnp.where(me == L - 1 - j, mapping, after[...])
+        mapping = times(mapping, got[L - 1 - j, R + W :])
     out[...] = half_of(total)
+    back[...] = half_of(mapping)
 
 
 def source_kernel(sections, got, before, states, inverse, arrow, out):
@@ -133,25 +161,6 @@
         out[n, T * G :] = total
 
 
-def maps_kernel(sections, backward, maps, chunk):
-    live = live_count(sections)
-    mapping = eye(F32)
-    for t in reversed(range(T)):
-        mapping = jnp.where(t < live, -times_t(mapping, backward[t]), mapping)
-        maps[t] = mapping
-    chunk[...] = mapping
-
-
-def group_maps_kernel(got, out, after):
-    me = near_index()
-    total = got[L - 1]
-    after[...] = eye(F32)
-    for j in reversed(range(L - 1)):
-        after[...] = jnp.where(me == j, total, after[...])
-        total = times(total, got[j])
-    out[...] = half_of(total)
-
-
 def arrive_kernel(sections, got, backward, sums, chunk):
     live = live_count(sections)
     whole = got[0]
@@ -166,26 +175,26 @@
     chunk[G:] = whole[T * G :]
 
 
-def back_group_kernel(got, maps, out, after):
+def back_group_kernel(got, maps, mapping, out, after):
     me = near_index()
     total = got[L - 1, :G]
     after[...] = jnp.zeros((G, W), F32)
     for j in reversed(range(L - 1)):
         after[...] = jnp.where(me == j, total, after[...])
-        total = times(total, maps[j]) + got[j, :G]
+        total = times(total, maps[j, R + W :]) + got[j, :G]
     whole = ((got[0, G:] + got[1, G:]) + got[2, G:]) + got[3, G:]
-    out[...] = half_of(jnp.concatenate([total, whole], 0))
+    out[:EDGE] = half_of(jnp.concatenate([total, whole], 0))
+    out[EDGE:] = mapping[...]
 
 
 def final_kernel(
-    sections, got, totals, after, after_map, sums, maps, side, tip_inverse, out, tip_out
+    sections, got, after, after_map, sums, maps, side, tip_inverse, out, tip_out
 ):
     group = lax.axis_index("zg")
     live = live_count(sections)
-    edge = (G + F) // 2
-    whole = got[1, edge - F :]
+    whole = got[1, EDGE - F : EDGE]
     for j in range(1, Q):
-        whole = whole + got[2 * j + 1, edge - F :]
+        whole = whole + got[2 * j + 1, EDGE - F : EDGE]
     gap = side[...] - whole[:, :R]
     tip = lax.dot_general(
         tip_inverse[...], gap, (((1,), (0,)), ((), ())), precision=HI, preferred_element_type=F32
@@ -196,11 +205,11 @@
     tip_out[...] = tip
 
     def offset(j):
-        return jnp.concatenate([got[2 * j], got[2 * j + 1, : edge - F]], 0)
+        return jnp.concatenate([got[2 * j, :EDGE], got[2 * j + 1, : EDGE - F]], 0)
 
     entry = jnp.where(group < Q - 1, offset(Q - 1), 0.0)
     for j in reversed(range(1, Q - 1)):
-        mapping = jnp.concatenate([totals[2 * j], totals[2 * j + 1]], 0)
+        mapping = jnp.concatenate([got[2 * j, EDGE:], got[2 * j + 1, EDGE:]], 0)
         entry = jnp.where(j > group, times(entry, mapping) + offset(j), entry)
     entry = times(entry, after_map[...]) + after[...]
     tip_high, tip_low = split(tip)
@@ -219,7 +228,7 @@
 HBM = pl.BlockSpec(memory_space=pltpu.HBM)
 
 
-def call(kernel, shapes, *args, own_copies=False, scratch=()):
+def call(kernel, shapes, *args, own_copies=False, scratch=(), grant=16 << 20):
     specs = [HBM if own_copies else SMEM if a.dtype == jnp.int32 else VMEM for a in args]
     shapes = [jax.ShapeDtypeStruct(s, F32) for s in shapes]
     return pl.pallas_call(
@@ -228,31 +237,37 @@
         in_specs=specs,
         out_specs=[VMEM] * len(shapes),
         scratch_shapes=scratch,
-        compiler_params=pltpu.CompilerParams(vmem_limit_bytes=16 << 20),
+        compiler_params=pltpu.CompilerParams(vmem_limit_bytes=grant),
+        name=kernel.__name__,
     )(*args)
 
 
 def on_device(
     sections, right_side, tip_side, diag_inverse, forward_coupling, backward_coupling, arrow_rows, tip_inverse
 ):
-    states, chunk = call(
+    states, maps, chunk = call(
         local_kernel,
-        [(T, R + W, W), (R + W, W)],
+        [(T, R + W, W), (T, W, W), (R + 2 * W, W)],
         sections,
         right_side,
         diag_inverse,
         forward_coupling,
+        backward_coupling,
         own_copies=True,
         scratch=(
             pltpu.SMEM(sections.shape, jnp.int32),
             pltpu.VMEM(right_side.shape, BF16),
             pltpu.VMEM(diag_inverse.shape, BF16),
             pltpu.VMEM(forward_coupling.shape, BF16),
-            pltpu.SemaphoreType.DMA((2 + 2 * T,)),
+            pltpu.VMEM(backward_coupling.shape, BF16),
+            pltpu.SemaphoreType.DMA((3 + 2 * T,)),
         ),
-    )
-    got = lax.all_gather(chunk, NEAR)
-    out, before = call(group_kernel, [((R + W) // 2, W), (R + W, W)], got)
+        grant=GRANT,
+    )
+    near = lax.all_gather(chunk, NEAR)
+    out, back, before, after_map = call(
+        group_kernel, [((R + W) // 2, W), (W // 2, W), (R + W, W), (W, W)], near
+    )
     got = lax.all_gather(out, FAR)
     (out,) = call(
         source_kernel,
@@ -265,20 +280,15 @@
         arrow_rows,
     )
     got = lax.all_to_all(out, SPACE, 0, 0, tiled=True)
-    maps, chunk = call(maps_kernel, [(T, W, W), (W, W)], sections, backward_coupling)
-    near_maps = lax.all_gather(chunk, NEAR)
-    out, after_map = call(group_maps_kernel, [(W // 2, W), (W, W)], near_maps)
-    far_maps = lax.all_gather(out, FAR)
     sums, chunk = call(arrive_kernel, [(T, G, W), (G + F, W)], sections, got, backward_coupling)
     got = lax.all_gather(chunk, NEAR)
-    out, after = call(back_group_kernel, [((G + F) // 2, W), (G, W)], got, near_maps)
+    out, after = call(back_group_kernel, [(EDGE + W // 2, W), (G, W)], got, near, back)
     got = lax.all_gather(out, FAR)
     solved, tip = call(
         final_kernel,
         [(T, R, W), (F, R)],
         sections,
         got,
-        far_maps,
         after,
         after_map,
         sums,

time: 119 us -> 118 us (level)
  blocking collectives: 87.6 us -> 104 us
  starting transfers between devices: 6.88 us -> 0 us
  waiting for transfers between devices: 6.03 us -> 0 us
  local copies, waits for them, and re-layouts: 5.85 us -> 1.02 us
    all_to_all x0 -> x1, blocking collectives: none -> 37.3 us  [on_device(): got = lax.all_to_all(out, SPACE, 0, 0, tiled=True)]
    all_gather x2 -> x1, blocking collectives: 20.2 us -> 7.29 us  [on_device(): got = lax.all_gather(chunk, NEAR)]
    all_gather x2 -> x1, blocking collectives: 25 us -> 13.9 us  [on_device(): near = lax.all_gather(chunk, NEAR)]
    all_to_all x1 -> x0, starting transfers between devices: 6.88 us -> none  [on_device(): got = lax.all_to_all(out, SPACE, 0, 0, tiled=True)]
    all_to_all x1 -> x0, waiting for transfers between devices: 6.03 us -> none  [on_device(): got = lax.all_to_all(out, SPACE, 0, 0, tiled=True)]
    unnamed x26 -> x16, local copies, waits for them, and re-layouts: 5.85 us -> 1.02 us
    all_gather x2, blocking collectives: 42.4 us -> 45.8 us  [on_device(): got = lax.all_gather(out, FAR)]
    pallas_call x8 -> x6, Pallas kernels: 11.5 us -> 11.8 us  [call(): pl.pallas_call(kernel, out_shape=shapes, in_specs=specs, out_specs=[VMEM]...]
  transfers between devices with their start and end apart: 1 -> 0, of which waited for: 1 -> 0; matrix products, arithmetic and copies ran while one was open for 0% -> 0% of each run, Pallas kernels for 1% -> 0%
where the time goes in v4:
time: 118 us
  blocking collectives  104 us (88%)
  Pallas kernels  11.8 us (10%)
    all_gather x2, blocking collectives, on_device(): got = lax.all_gather(out, FAR)  45.8 us
    all_to_all x1, blocking collectives, on_device(): got = lax.all_to_all(out, SPACE, 0, 0, tiled=True)  37.3 us
    all_gather x1, blocking collectives, on_device(): near = lax.all_gather(chunk, NEAR)  13.9 us
    pallas_call x6, Pallas kernels, call(): pl.pallas_call(kernel, out_shape=shapes, in_specs=specs, out_specs=[VMEM]...  11.8 us
    all_gather x1, blocking collectives, on_device(): got = lax.all_gather(chunk, NEAR)  7.29 us

profile of v4, /device:TPU:1, one launch (start us, length us, event | category | flops | bytes accessed | tf_op | source)
XLA Modules:
  0.0 117.8 jit_solution(34582544979459298)
XLA Ops:
  0.6 0.0 copy-start.5
  0.6 0.0 copy-start.4
  0.7 4.1 %local_kernel.1 = (f32[4,192,128]{2,1,0:T(8,128)}, f32[4,128,128]{2,1,0:T(8,128)}, f32[320,128]{1,0:T(8,128)}) custom-call(s32[32]{0:T(128)} %sections.5, bf16[4,64,2048]{2,1,0:T(8,128)(2,1)} %side_in.1, bf16[4,128,2048]{2,1,0:T(8,128)(2,1)} %inverse.1, bf16[4,128,128]{2,1,0:T(8,128)(2,1)} %forward_in.1, bf16[4,128,128]{2,1,0:T(8,128)(2,1)} %backward.1), custom_call_target="tpu_custom_call" | custom-call | tf_op jit(solution)/shard_map/local_kernel/pallas_call | solution.py:234
  4.8 0.0 copy-start
  4.8 13.9 %all-gather = f32[1280,128]{1,0:T(8,128)S(1)} all-gather(f32[320,128]{1,0:T(8,128)} %get-tuple-element.15), channel_id=2, replica_groups=mesh['zg'=8,'zp'=2,'core'=2,'x'=4,'y'=4] {'zp','core'}, dimensions={0}, use_global_device_ids=true | all-gather | bytes 819200 | tf_op jit(solution)/shard_map/all_gather | solution.py:267
  18.7 0.5 group_kernel.1
  19.2 24.8 %all-gather.1 = f32[1536,128]{1,0:T(8,128)S(1)} all-gather(f32[96,128]{1,0:T(8,128)S(1)} %get-tuple-element.16), channel_id=3, replica_groups=mesh['zg'=8,'zp'=2,'core'=2,'x'=4,'y'=4] {'zg','core'}, dimensions={0}, use_global_device_ids=true | all-gather | bytes 835584 | tf_op jit(solution)/shard_map/all_gather | solution.py:271
  44.0 0.0 copy-done.5
  44.0 0.0 copy-done.4
  44.0 0.0 copy-done
  44.0 0.0 copy-start.2
  44.0 1.0 copy-done.2
  45.0 2.8 %source_kernel.1 = f32[16,296,128]{2,1,0:T(8,128)S(1)} custom-call(s32[32]{0:T(128)S(1)} %copy-done.5, f32[16,96,128]{2,1,0:T(8,128)S(1)} %bitcast.9, f32[192,128]{1,0:T(8,128)S(1)} %get-tuple-element.17.before, f32[4,192,128]{2,1,0:T(8,128)S(1)} %copy-done.2, bf16[4,128,2048]{2,1,0:T(8,128)(2,1)S(1)} %copy-done, bf16[4,8,128]{2,1,0:T(8,128)(2,1)S(1)} %copy-done.4), custom_call_target="tpu_custom_call" | custom-call | tf_op jit(solution)/shard_map/source_kernel/pallas_call | solution.py:234
  47.8 0.0 copy-start.1
  47.8 37.3 %all_to_all.5.got = f32[16,296,128]{2,1,0:T(8,128)S(1)} all-to-all(f32[16,296,128]{2,1,0:T(8,128)S(1)} %source_kernel.1), channel_id=1, replica_groups=mesh['zg'=8,'zp'=2,'core'=2,'x'=4,'y'=4] {'x','y'}, dimensions={0} | all-to-all | bytes 4849664 | tf_op jit(solution)/shard_map/all_to_all | solution.py:282
  85.1 0.0 copy-done.1
  85.1 0.0 copy-start.3
  85.1 0.0 copy-start.6
  85.1 0.0 copy-start.7
  85.1 1.1 arrive_kernel.1
  86.2 7.3 %all-gather.2 = f32[320,128]{1,0:T(8,128)S(1)} all-gather(f32[80,128]{1,0:T(8,128)S(1)} %get-tuple-element.19), channel_id=4, replica_groups=mesh['zg'=8,'zp'=2,'core'=2,'x'=4,'y'=4] {'zp','core'}, dimensions={0}, use_global_device_ids=true | all-gather | bytes 204800 | tf_op jit(solution)/shard_map/all_gather | solution.py:284
  93.5 0.4 back_group_kernel.1
  93.9 21.0 %all-gather.3 = f32[1664,128]{1,0:T(8,128)S(1)} all-gather(f32[104,128]{1,0:T(8,128)S(1)} %get-tuple-element.21), channel_id=5, replica_groups=mesh['zg'=8,'zp'=2,'core'=2,'x'=4,'y'=4] {'zg','core'}, dimensions={0}, use_global_device_ids=true | all-gather | bytes 905216 | tf_op jit(solution)/shard_map/all_gather | solution.py:286
  114.9 0.0 copy-done.3
  114.9 0.0 copy-done.6
  114.9 0.0 copy-done.7
  114.9 2.9 %final_kernel.1 = (f32[4,64,128]{2,1,0:T(8,128)}, f32[8,64]{1,0:T(8,128)}) custom-call(s32[32]{0:T(128)S(1)} %copy-done.5, f32[16,104,128]{2,1,0:T(8,128)S(1)} %bitcast.8, f32[72,128]{1,0:T(8,128)S(1)} %get-tuple-element.22.after, f32[128,128]{1,0:T(8,128)S(1)} %get-tuple-element.23.after_map, f32[4,72,128]{2,1,0:T(8,128)S(1)} %get-tuple-element.24.sums, ...), custom_call_target="tpu_custom_call" | custom-call | tf_op jit(solution)/shard_map/final_kernel/pallas_call | solution.py:234
Async XLA Ops:
  0.6 43.4 %copy-start.5 = (s32[32]{0:T(128)S(1)}, s32[32]{0:T(128)}, u32[]{:S(2)}) copy-start(s32[32]{0:T(128)} %sections.5) | copy-start | bytes 388
  0.6 43.4 %copy-start.4 = (bf16[4,8,128]{2,1,0:T(8,128)(2,1)S(1)}, bf16[4,8,128]{2,1,0:T(8,128)(2,1)}, u32[]{:S(2)}) copy-start(bf16[4,8,128]{2,1,0:T(8,128)(2,1)} %arrow.1) | copy-start | bytes 24580
  4.8 39.2 %copy-start = (bf16[4,128,2048]{2,1,0:T(8,128)(2,1)S(1)}, bf16[4,128,2048]{2,1,0:T(8,128)(2,1)}, u32[]{:S(2)}) copy-start(bf16[4,128,2048]{2,1,0:T(8,128)(2,1)} %inverse.1) | copy-start | bytes 6291460
  44.0 1.0 copy-start.2
  47.8 37.3 %copy-start.1 = (bf16[4,128,128]{2,1,0:T(8,128)(2,1)S(1)}, bf16[4,128,128]{2,1,0:T(8,128)(2,1)}, u32[]{:S(2)}) copy-start(bf16[4,128,128]{2,1,0:T(8,128)(2,1)} %backward.1) | copy-start | bytes 393220
  85.1 29.8 %copy-start.3 = (f32[4,128,128]{2,1,0:T(8,128)S(1)}, f32[4,128,128]{2,1,0:T(8,128)}, u32[]{:S(2)}) copy-start(f32[4,128,128]{2,1,0:T(8,128)} %get-tuple-element.25.maps) | copy-start | bytes 786436
  85.1 29.8 %copy-start.6 = (f32[64,8]{0,1:T(8,128)S(1)}, f32[64,8]{0,1:T(8,128)}, u32[]{:S(2)}) copy-start(f32[64,8]{0,1:T(8,128)} %param.10) | copy-start | bytes 6148
  85.1 29.8 %copy-start.7 = (f32[8,8]{1,0:T(8,128)S(1)}, f32[8,8]{1,0:T(8,128)}, u32[]{:S(2)}) copy-start(f32[8,8]{1,0:T(8,128)} %tip_inverse.1) | copy-start | bytes 772

commit v5 on v4

--- a/solution.py
+++ b/solution.py
@@ -23,7 +23,6 @@
 L = 4
 Q = 8
 EDGE = (G + F) // 2
-GRANT = 66_000_000
 HI = lax.Precision.HIGHEST
 
 
@@ -61,9 +60,22 @@
     return sections[lax.axis_index("zg") * L + near_index()]
 
 
-def join(first, then):
-    out = times(first, then[R : R + W])
-    return jnp.concatenate([out[:R] + then[:R], out[R:]], 0)
+def join(first, then, rows=R):
+    out = times(first, then[rows:])
+    return jnp.concatenate([out[:rows] + then[:rows], out[rows:]], 0)
+
+
+def offset_of(parts, rows):
+    ahead = times(parts[0][:rows], parts[1][rows:]) + parts[1][:rows]
+    middle = join(parts[2], parts[3], rows)
+    behind = join(join(parts[4], parts[5], rows), parts[6], rows)
+    ahead = times(ahead, middle[rows:]) + middle[:rows]
+    return times(ahead, behind[rows:]) + behind[:rows]
+
+
+def kept(flag, part, rows):
+    neutral = jnp.concatenate([jnp.zeros((rows, W), F32), eye(F32)], 0)
+    return jnp.where(flag, part, neutral)
 
 
 def half_of(x):
@@ -80,11 +92,11 @@
     states,
     maps,
     chunk,
+    inverse,
+    backward,
     sections,
     side,
-    inverse,
     forward,
-    backward,
     sems,
 ):
     copies = [
@@ -105,20 +117,23 @@
         mapping = jnp.where(t < live, -times_t(mapping, backward[t]), mapping)
         maps[t] = mapping
     chunk[R + W :] = mapping
+    mapping = -dot(eye(BF16), forward[0], (1, 1))
+    for t in range(T):
+        if t > 0:
+            mapping = jnp.where(t < live, -times_t(mapping, forward[t]), mapping)
+        states[t, R:] = mapping
+    chunk[R : R + W] = mapping
     state = None
     for t in range(T):
         copies[3 + 2 * t].wait()
         copies[4 + 2 * t].wait()
         driven = dot(side[t], inverse[t], (1, 1))
         if t == 0:
-            state = jnp.concatenate([driven, -dot(eye(BF16), forward[0], (1, 1))], 0)
+            state = driven
         else:
-            moved = times_t(state, forward[t])
-            state = jnp.where(
-                t < live, jnp.concatenate([driven - moved[:R], -moved[R:]], 0), state
-            )
-        states[t] = state
-    chunk[: R + W] = state
+            state = jnp.where(t < live, driven - times_t(state, forward[t]), state)
+        states[t, :R] = state
+    chunk[:R] = state
 
 
 def group_kernel(got, out, back, before, after):
@@ -139,16 +154,16 @@
 def source_kernel(sections, got, before, states, inverse, arrow, out):
     group = lax.axis_index("zg")
     live = live_count(sections)
-    entry = jnp.where(group > 0, got[0, :R], 0.0)
-    for j in range(1, Q - 1):
-        mapping = jnp.concatenate([got[2 * j, R:], got[2 * j + 1]], 0)
-        entry = jnp.where(j < group, times(entry, mapping) + got[2 * j, :R], entry)
+    parts = [
+        kept(j < group, jnp.concatenate([got[2 * j], got[2 * j + 1]], 0), R) for j in range(Q - 1)
+    ]
+    entry = offset_of(parts, R)
     entry = times(entry, before[R:]) + before[:R]
+    moved = times(entry, jnp.concatenate([states[t, R:] for t in range(T)], 1))
     total = jnp.zeros((F, W), F32)
     pad = jnp.zeros((W - R, W), BF16)
     for t in range(T):
-        state = states[t]
-        state = jnp.where(t < live, state[:R] + times(entry, state[R:]), 0.0)
+        state = jnp.where(t < live, states[t, :R] + moved[:, t * W : (t + 1) * W], 0.0)
         high, low = split(state)
         total += dot(arrow[t], jnp.concatenate([high, pad], 0), (1, 1))
         rows = jnp.concatenate([high, low, arrow[t], jnp.zeros((F, W), BF16)], 0)
@@ -204,23 +219,24 @@
     )
     tip_out[...] = tip
 
-    def offset(j):
-        return jnp.concatenate([got[2 * j, :EDGE], got[2 * j + 1, : EDGE - F]], 0)
-
-    entry = jnp.where(group < Q - 1, offset(Q - 1), 0.0)
-    for j in reversed(range(1, Q - 1)):
-        mapping = jnp.concatenate([got[2 * j, EDGE:], got[2 * j + 1, EDGE:]], 0)
-        entry = jnp.where(j > group, times(entry, mapping) + offset(j), entry)
+    parts = []
+    for j in reversed(range(1, Q)):
+        first, second = got[2 * j], got[2 * j + 1]
+        part = [first[:EDGE], second[: EDGE - F], first[EDGE:], second[EDGE:]]
+        parts.append(kept(j > group, jnp.concatenate(part, 0), G))
+    entry = offset_of(parts, G)
     entry = times(entry, after_map[...]) + after[...]
+    state = times(entry, jnp.concatenate([maps[t] for t in range(T)], 1))
+    state = state + jnp.concatenate([sums[t] for t in range(T)], 1)
     tip_high, tip_low = split(tip)
     weights = jnp.concatenate(
         [tip_high.astype(F32), tip_low.astype(F32), tip_high.astype(F32)], 0
     ).astype(BF16)
-    for t in range(T):
-        state = sums[t] + times(entry, maps[t])
-        high, low = split(state[R:])
-        parts = jnp.concatenate([high.astype(F32), high.astype(F32), low.astype(F32)], 0).astype(BF16)
-        out[t] = jnp.where(t < live, state[:R] - dot(weights, parts, (0, 0)), 0.0)
+    high, low = split(state[R:])
+    fixed = jnp.concatenate([high.astype(F32), high.astype(F32), low.astype(F32)], 0).astype(BF16)
+    state = state[:R] - dot(weights, fixed, (0, 0))
+    for t in range(T):
+        out[t] = jnp.where(t < live, state[:, t * W : (t + 1) * W], 0.0)
 
 
 VMEM = pl.BlockSpec(memory_space=pltpu.VMEM)
@@ -228,16 +244,18 @@
 HBM = pl.BlockSpec(memory_space=pltpu.HBM)
 
 
-def call(kernel, shapes, *args, own_copies=False, scratch=(), grant=16 << 20):
+def call(kernel, shapes, *args, own_copies=False, scratch=()):
     specs = [HBM if own_copies else SMEM if a.dtype == jnp.int32 else VMEM for a in args]
-    shapes = [jax.ShapeDtypeStruct(s, F32) for s in shapes]
+    shapes = [s if hasattr(s, "dtype") else jax.ShapeDtypeStruct(s, F32) for s in shapes]
+    if own_copies:
+        args = [pltpu.with_memory_space_constraint(a, pltpu.HBM) for a in args]
     return pl.pallas_call(
         kernel,
         out_shape=shapes,
         in_specs=specs,
         out_specs=[VMEM] * len(shapes),
         scratch_shapes=scratch,
-        compiler_params=pltpu.CompilerParams(vmem_limit_bytes=grant),
+        compiler_params=pltpu.CompilerParams(vmem_limit_bytes=16 << 20),
         name=kernel.__name__,
     )(*args)
 
@@ -245,9 +263,10 @@
 def on_device(
     sections, right_side, tip_side, diag_inverse, forward_coupling, backward_coupling, arrow_rows, tip_inverse
 ):
-    states, maps, chunk = call(
+    kept_inputs = [jax.ShapeDtypeStruct(a.shape, BF16) for a in (diag_inverse, backward_coupling)]
+    states, maps, chunk, inverse, backward = call(
         local_kernel,
-        [(T, R + W, W), (T, W, W), (R + 2 * W, W)],
+        [(T, R + W, W), (T, W, W), (R + 2 * W, W)] + kept_inputs,
         sections,
         right_side,
         diag_inverse,
@@ -257,12 +276,9 @@
         scratch=(
             pltpu.SMEM(sections.shape, jnp.int32),
             pltpu.VMEM(right_side.shape, BF16),
-            pltpu.VMEM(diag_inverse.shape, BF16),
             pltpu.VMEM(forward_coupling.shape, BF16),
-            pltpu.VMEM(backward_coupling.shape, BF16),
             pltpu.SemaphoreType.DMA((3 + 2 * T,)),
         ),
-        grant=GRANT,
     )
     near = lax.all_gather(chunk, NEAR)
     out, back, before, after_map = call(
@@ -276,11 +292,11 @@
         got,
         before,
         states,
-        diag_inverse,
+        inverse,
         arrow_rows,
     )
     got = lax.all_to_all(out, SPACE, 0, 0, tiled=True)
-    sums, chunk = call(arrive_kernel, [(T, G, W), (G + F, W)], sections, got, backward_coupling)
+    sums, chunk = call(arrive_kernel, [(T, G, W), (G + F, W)], sections, got, backward)
     got = lax.all_gather(chunk, NEAR)
     out, after = call(back_group_kernel, [(EDGE + W // 2, W), (G, W)], got, near, back)
     got = lax.all_gather(out, FAR)

time: 118 us -> 115 us (0.975)
  Pallas kernels: 11.8 us -> 10.1 us
    pallas_call x6, Pallas kernels: 11.8 us -> 10.1 us  [call(): pl.pallas_call(kernel, out_shape=shapes, in_specs=specs, out_specs=[VMEM]...]
where the time goes in v5:
time: 115 us
  blocking collectives  104 us (90%)
  Pallas kernels  10.1 us (9%)
    all_gather x2, blocking collectives, on_device(): got = lax.all_gather(out, FAR)  45.8 us
    all_to_all x1, blocking collectives, on_device(): got = lax.all_to_all(out, SPACE, 0, 0, tiled=True)  37.2 us
    all_gather x1, blocking collectives, on_device(): near = lax.all_gather(chunk, NEAR)  13.5 us
    pallas_call x6, Pallas kernels, call(): pl.pallas_call(kernel, out_shape=shapes, in_specs=specs, out_specs=[VMEM]...  10.1 us
    all_gather x1, blocking collectives, on_device(): got = lax.all_gather(chunk, NEAR)  7.3 us

profile of v5, /device:TPU:1, one launch (start us, length us, event | category | flops | bytes accessed | tf_op | source)
XLA Modules:
  0.0 114.6 jit_solution(2527093695238064414)
XLA Ops:
  0.6 0.0 copy-start.1
  0.6 0.0 copy-start
  0.7 3.6 %local_kernel.1 = (f32[4,192,128]{2,1,0:T(8,128)S(1)}, f32[4,128,128]{2,1,0:T(8,128)S(1)}, f32[320,128]{1,0:T(8,128)S(1)}, bf16[4,128,2048]{2,1,0:T(8,128)(2,1)S(1)}, bf16[4,128,128]{2,1,0:T(8,128)(2,1)S(1)}) custom-call(s32[32]{0:T(128)} %sections.5, bf16[4,64,2048]{2,1,0:T(8,128)(2,1)} %side_in.1, bf16[4,128,2048]{2,1,0:T(8,128)(2,1)} %inverse_in.1, ...), custom_call_target="tpu_custom_call" | custom-call | tf_op jit(solution)/shard_map/local_kernel/pallas_call | solution.py:252
  4.2 13.5 %all-gather = f32[1280,128]{1,0:T(8,128)S(1)} all-gather(f32[320,128]{1,0:T(8,128)S(1)} %get-tuple-element.17), channel_id=2, replica_groups=mesh['zg'=8,'zp'=2,'core'=2,'x'=4,'y'=4] {'zp','core'}, dimensions={0}, use_global_device_ids=true | all-gather | bytes 819200 | tf_op jit(solution)/shard_map/all_gather | solution.py:283
  17.8 0.5 group_kernel.1
  18.3 24.8 %all-gather.1 = f32[1536,128]{1,0:T(8,128)S(1)} all-gather(f32[96,128]{1,0:T(8,128)S(1)} %get-tuple-element.18), channel_id=3, replica_groups=mesh['zg'=8,'zp'=2,'core'=2,'x'=4,'y'=4] {'zg','core'}, dimensions={0}, use_global_device_ids=true | all-gather | bytes 835584 | tf_op jit(solution)/shard_map/all_gather | solution.py:287
  43.1 0.0 copy-done.1
  43.1 0.0 copy-done
  43.1 2.2 %source_kernel.1 = f32[16,296,128]{2,1,0:T(8,128)S(1)} custom-call(s32[32]{0:T(128)S(1)} %copy-done.1, f32[16,96,128]{2,1,0:T(8,128)S(1)} %bitcast.9, f32[192,128]{1,0:T(8,128)S(1)} %get-tuple-element.19.before, f32[4,192,128]{2,1,0:T(8,128)S(1)} %get-tuple-element.20.states, bf16[4,128,2048]{2,1,0:T(8,128)(2,1)S(1)} %get-tuple-element.21.inverse, ...), custom_call_target="tpu_custom_call" | custom-call | tf_op jit(solution)/shard_map/source_kernel/pallas_call | solution.py:252
  45.3 37.2 %all_to_all.5.got = f32[16,296,128]{2,1,0:T(8,128)S(1)} all-to-all(f32[16,296,128]{2,1,0:T(8,128)S(1)} %source_kernel.1), channel_id=1, replica_groups=mesh['zg'=8,'zp'=2,'core'=2,'x'=4,'y'=4] {'x','y'}, dimensions={0} | all-to-all | bytes 4849664 | tf_op jit(solution)/shard_map/all_to_all | solution.py:298
  82.4 0.0 copy-start.2
  82.4 0.0 copy-start.3
  82.4 1.1 arrive_kernel.1
  83.5 7.3 %all-gather.2 = f32[320,128]{1,0:T(8,128)S(1)} all-gather(f32[80,128]{1,0:T(8,128)S(1)} %get-tuple-element.23), channel_id=4, replica_groups=mesh['zg'=8,'zp'=2,'core'=2,'x'=4,'y'=4] {'zp','core'}, dimensions={0}, use_global_device_ids=true | all-gather | bytes 204800 | tf_op jit(solution)/shard_map/all_gather | solution.py:300
  90.8 0.4 back_group_kernel.1
  91.2 21.0 %all-gather.3 = f32[1664,128]{1,0:T(8,128)S(1)} all-gather(f32[104,128]{1,0:T(8,128)S(1)} %get-tuple-element.25), channel_id=5, replica_groups=mesh['zg'=8,'zp'=2,'core'=2,'x'=4,'y'=4] {'zg','core'}, dimensions={0}, use_global_device_ids=true | all-gather | bytes 905216 | tf_op jit(solution)/shard_map/all_gather | solution.py:302
  112.2 0.0 copy-done.2
  112.2 0.0 copy-done.3
  112.2 2.4 %final_kernel.1 = (f32[4,64,128]{2,1,0:T(8,128)}, f32[8,64]{1,0:T(8,128)}) custom-call(s32[32]{0:T(128)S(1)} %copy-done.1, f32[16,104,128]{2,1,0:T(8,128)S(1)} %bitcast.8, f32[72,128]{1,0:T(8,128)S(1)} %get-tuple-element.26.after, f32[128,128]{1,0:T(8,128)S(1)} %get-tuple-element.27.after_map, f32[4,72,128]{2,1,0:T(8,128)S(1)} %get-tuple-element.28.sums, ...), custom_call_target="tpu_custom_call" | custom-call | tf_op jit(solution)/shard_map/final_kernel/pallas_call | solution.py:252
Async XLA Ops:
  0.6 42.5 %copy-start.1 = (s32[32]{0:T(128)S(1)}, s32[32]{0:T(128)}, u32[]{:S(2)}) copy-start(s32[32]{0:T(128)} %sections.5) | copy-start | bytes 388
  0.6 42.5 %copy-start = (bf16[4,8,128]{2,1,0:T(8,128)(2,1)S(1)}, bf16[4,8,128]{2,1,0:T(8,128)(2,1)}, u32[]{:S(2)}) copy-start(bf16[4,8,128]{2,1,0:T(8,128)(2,1)} %arrow.1) | copy-start | bytes 24580
  82.4 29.8 %copy-start.2 = (f32[64,8]{0,1:T(8,128)S(1)}, f32[64,8]{0,1:T(8,128)}, u32[]{:S(2)}) copy-start(f32[64,8]{0,1:T(8,128)} %param.10) | copy-start | bytes 6148
  82.4 29.8 %copy-start.3 = (f32[8,8]{1,0:T(8,128)S(1)}, f32[8,8]{1,0:T(8,128)}, u32[]{:S(2)}) copy-start(f32[8,8]{1,0:T(8,128)} %tip_inverse.1) | copy-start | bytes 772

commit v6 on v5

--- a/solution.py
+++ b/solution.py
@@ -21,6 +21,8 @@
 N = 16
 G = R + F
 L = 4
+K = 4
+PLANE = ("core",) + SPACE
 Q = 8
 EDGE = (G + F) // 2
 HI = lax.Precision.HIGHEST
@@ -153,6 +155,7 @@
 
 def source_kernel(sections, got, before, states, inverse, arrow, out):
     group = lax.axis_index("zg")
+    core = lax.axis_index("core")
     live = live_count(sections)
     parts = [
         kept(j < group, jnp.concatenate([got[2 * j], got[2 * j + 1]], 0), R) for j in range(Q - 1)
@@ -170,17 +173,21 @@
         terms = dot(rows, inverse[t], (1, 0))
         for n in range(N):
             cols = slice(n * W, (n + 1) * W)
-            out[n, t * G : t * G + R] = terms[:R, cols] + terms[R : 2 * R, cols]
-            out[n, t * G + R : (t + 1) * G] = terms[2 * R : 2 * R + F, cols]
+            slot = jnp.where(core == 0, n, n % K * K + n // K)
+            out[slot, t * G : t * G + R] = terms[:R, cols] + terms[R : 2 * R, cols]
+            out[slot, t * G + R : (t + 1) * G] = terms[2 * R : 2 * R + F, cols]
     for n in range(N):
         out[n, T * G :] = total
 
 
+def fold_kernel(got, out):
+    for n in range(K):
+        out[n] = (got[n] + got[K + n]) + (got[2 * K + n] + got[3 * K + n])
+
+
 def arrive_kernel(sections, got, backward, sums, chunk):
     live = live_count(sections)
-    whole = got[0]
-    for n in range(1, N):
-        whole = whole + got[n]
+    whole = (got[0] + got[1]) + (got[2] + got[3])
     state = jnp.zeros((G, W), F32)
     for t in reversed(range(T)):
         source = whole[t * G : (t + 1) * G]
@@ -258,6 +265,15 @@
         compiler_params=pltpu.CompilerParams(vmem_limit_bytes=16 << 20),
         name=kernel.__name__,
     )(*args)
+
+
+def along(stage):
+    groups = []
+    for core in range(2):
+        for line in range(K):
+            steps = [k * K + line if core == stage else line * K + k for k in range(K)]
+            groups.append([core * N + step for step in steps])
+    return groups
 
 
 def on_device(
@@ -295,7 +311,9 @@
         inverse,
         arrow_rows,
     )
-    got = lax.all_to_all(out, SPACE, 0, 0, tiled=True)
+    got = lax.all_to_all(out, PLANE, 0, 0, axis_index_groups=along(0), tiled=True)
+    (out,) = call(fold_kernel, [(K, T * G + F, W)], got)
+    got = lax.all_to_all(out, PLANE, 0, 0, axis_index_groups=along(1), tiled=True)
     sums, chunk = call(arrive_kernel, [(T, G, W), (G + F, W)], sections, got, backward)
     got = lax.all_gather(chunk, NEAR)
     out, after = call(back_group_kernel, [(EDGE + W // 2, W), (G, W)], got, near, back)

time: 115 us -> 111 us (0.965)
  blocking collectives: 104 us -> 100 us
    all_to_all x1 -> x2, blocking collectives: 37.2 us -> 32.4 us  [the longest x1 21.1 us: on_device(): lax.all_to_all(out, PLANE, 0, 0, axis_index_groups=along(0), tiled=True)]
    pallas_call x6 -> x7, Pallas kernels: 10.1 us -> 10.2 us  [call(): pl.pallas_call(kernel, out_shape=shapes, in_specs=specs, out_specs=[VMEM]...]
where the time goes in v6:
time: 111 us
  blocking collectives  100 us (90%)
  Pallas kernels  10.2 us (9%)
    all_gather x2, blocking collectives, on_device(): got = lax.all_gather(out, FAR)  45.8 us
    all_to_all x1, blocking collectives, on_device(): lax.all_to_all(out, PLANE, 0, 0, axis_index_groups=along(0), tiled=True)  21.1 us
    all_gather x1, blocking collectives, on_device(): near = lax.all_gather(chunk, NEAR)  13.5 us
    all_to_all x1, blocking collectives, on_device(): lax.all_to_all(out, PLANE, 0, 0, axis_index_groups=along(1), tiled=True)  11.3 us
    pallas_call x7, Pallas kernels, call(): pl.pallas_call(kernel, out_shape=shapes, in_specs=specs, out_specs=[VMEM]...  10.2 us
    all_gather x1, blocking collectives, on_device(): got = lax.all_gather(chunk, NEAR)  8.28 us

profile of v6, /device:TPU:1, one launch (start us, length us, event | category | flops | bytes accessed | tf_op | source)
XLA Modules:
  0.0 110.9 jit_solution(1289815093065909872)
XLA Ops:
  0.6 0.0 copy-start
  0.6 0.0 copy-start.1
  0.7 3.6 %local_kernel.1 = (f32[4,192,128]{2,1,0:T(8,128)S(1)}, f32[4,128,128]{2,1,0:T(8,128)S(1)}, f32[320,128]{1,0:T(8,128)S(1)}, bf16[4,128,2048]{2,1,0:T(8,128)(2,1)S(1)}, bf16[4,128,128]{2,1,0:T(8,128)(2,1)S(1)}) custom-call(s32[32]{0:T(128)} %sections.5, bf16[4,64,2048]{2,1,0:T(8,128)(2,1)} %side_in.1, bf16[4,128,2048]{2,1,0:T(8,128)(2,1)} %inverse_in.1, ...), custom_call_target="tpu_custom_call" | custom-call | tf_op jit(solution)/shard_map/local_kernel/pallas_call | solution.py:259
  4.2 13.5 %all-gather = f32[1280,128]{1,0:T(8,128)S(1)} all-gather(f32[320,128]{1,0:T(8,128)S(1)} %get-tuple-element.17), channel_id=2, replica_groups=mesh['zg'=8,'zp'=2,'core'=2,'x'=4,'y'=4] {'zp','core'}, dimensions={0}, use_global_device_ids=true | all-gather | bytes 819200 | tf_op jit(solution)/shard_map/all_gather | solution.py:299
  17.8 0.5 group_kernel.1
  18.3 24.8 %all-gather.1 = f32[1536,128]{1,0:T(8,128)S(1)} all-gather(f32[96,128]{1,0:T(8,128)S(1)} %get-tuple-element.18), channel_id=3, replica_groups=mesh['zg'=8,'zp'=2,'core'=2,'x'=4,'y'=4] {'zg','core'}, dimensions={0}, use_global_device_ids=true | all-gather | bytes 835584 | tf_op jit(solution)/shard_map/all_gather | solution.py:303
  43.1 0.0 copy-done
  43.1 0.0 copy-done.1
  43.1 2.2 %source_kernel.1 = f32[16,296,128]{2,1,0:T(8,128)S(1)} custom-call(s32[32]{0:T(128)S(1)} %copy-done, f32[16,96,128]{2,1,0:T(8,128)S(1)} %bitcast.9, f32[192,128]{1,0:T(8,128)S(1)} %get-tuple-element.19.before, f32[4,192,128]{2,1,0:T(8,128)S(1)} %get-tuple-element.20.states, bf16[4,128,2048]{2,1,0:T(8,128)(2,1)S(1)} %get-tuple-element.21.inverse, ...), custom_call_target="tpu_custom_call" | custom-call | tf_op jit(solution)/shard_map/source_kernel/pallas_call | solution.py:259
  45.3 21.1 %all_to_all.10.got = f32[16,296,128]{2,1,0:T(8,128)S(1)} all-to-all(f32[16,296,128]{2,1,0:T(8,128)S(1)} %source_kernel.1), channel_id=1, replica_groups={{0,4,8,12},{1,5,9,13},{2,6,10,14},{3,7,11,15},{16,17,18,19},{20,21,22,2..., dimensions={0} | all-to-all | bytes 4849664 | tf_op jit(solution)/shard_map/all_to_all | solution.py:314
  66.4 0.1 fold_kernel.1
  66.5 0.0 copy-start.2
  66.5 0.0 copy-start.3
  66.5 11.3 %all_to_all.11.got = f32[4,296,128]{2,1,0:T(8,128)S(1)} all-to-all(f32[4,296,128]{2,1,0:T(8,128)S(1)} %fold_kernel.1), channel_id=1, replica_groups={{0,1,2,3},{4,5,6,7},{8,9,10,11},{12,13,14,15},{16,20,24,28},{17,21,25,2..., dimensions={0} | all-to-all | bytes 1212416 | tf_op jit(solution)/shard_map/all_to_all | solution.py:316
  77.8 1.1 arrive_kernel.1
  78.8 8.3 %all-gather.2 = f32[320,128]{1,0:T(8,128)S(1)} all-gather(f32[80,128]{1,0:T(8,128)S(1)} %get-tuple-element.23), channel_id=4, replica_groups=mesh['zg'=8,'zp'=2,'core'=2,'x'=4,'y'=4] {'zp','core'}, dimensions={0}, use_global_device_ids=true | all-gather | bytes 204800 | tf_op jit(solution)/shard_map/all_gather | solution.py:318
  87.1 0.4 back_group_kernel.1
  87.5 21.0 %all-gather.3 = f32[1664,128]{1,0:T(8,128)S(1)} all-gather(f32[104,128]{1,0:T(8,128)S(1)} %get-tuple-element.25), channel_id=5, replica_groups=mesh['zg'=8,'zp'=2,'core'=2,'x'=4,'y'=4] {'zg','core'}, dimensions={0}, use_global_device_ids=true | all-gather | bytes 905216 | tf_op jit(solution)/shard_map/all_gather | solution.py:320
  108.5 0.0 copy-done.2
  108.5 0.0 copy-done.3
  108.5 2.4 %final_kernel.1 = (f32[4,64,128]{2,1,0:T(8,128)}, f32[8,64]{1,0:T(8,128)}) custom-call(s32[32]{0:T(128)S(1)} %copy-done, f32[16,104,128]{2,1,0:T(8,128)S(1)} %bitcast.8, f32[72,128]{1,0:T(8,128)S(1)} %get-tuple-element.26.after, f32[128,128]{1,0:T(8,128)S(1)} %get-tuple-element.27.after_map, f32[4,72,128]{2,1,0:T(8,128)S(1)} %get-tuple-element.28.sums, ...), custom_call_target="tpu_custom_call" | custom-call | tf_op jit(solution)/shard_map/final_kernel/pallas_call | solution.py:259
Async XLA Ops:
  0.6 42.5 %copy-start = (s32[32]{0:T(128)S(1)}, s32[32]{0:T(128)}, u32[]{:S(2)}) copy-start(s32[32]{0:T(128)} %sections.5) | copy-start | bytes 388
  0.6 42.5 %copy-start.1 = (bf16[4,8,128]{2,1,0:T(8,128)(2,1)S(1)}, bf16[4,8,128]{2,1,0:T(8,128)(2,1)}, u32[]{:S(2)}) copy-start(bf16[4,8,128]{2,1,0:T(8,128)(2,1)} %arrow.1) | copy-start | bytes 24580
  66.5 42.0 %copy-start.2 = (f32[64,8]{0,1:T(8,128)S(1)}, f32[64,8]{0,1:T(8,128)}, u32[]{:S(2)}) copy-start(f32[64,8]{0,1:T(8,128)} %param.10) | copy-start | bytes 6148
  66.5 42.0 %copy-start.3 = (f32[8,8]{1,0:T(8,128)S(1)}, f32[8,8]{1,0:T(8,128)}, u32[]{:S(2)}) copy-start(f32[8,8]{1,0:T(8,128)} %tip_inverse.1) | copy-start | bytes 772

commit v7 on v6

--- a/solution.py
+++ b/solution.py
@@ -94,6 +94,7 @@
     states,
     maps,
     chunk,
+    counts,
     inverse,
     backward,
     sections,
@@ -114,6 +115,7 @@
     for copy in copies[:3]:
         copy.wait()
     live = live_count(sections)
+    counts[...] = jnp.full((F, W), live, jnp.int32).astype(F32)
     mapping = eye(F32)
     for t in reversed(range(T)):
         mapping = jnp.where(t < live, -times_t(mapping, backward[t]), mapping)
@@ -153,10 +155,10 @@
     back[...] = half_of(mapping)
 
 
-def source_kernel(sections, got, before, states, inverse, arrow, out):
+def source_kernel(counts, got, before, states, inverse, arrow, out):
     group = lax.axis_index("zg")
     core = lax.axis_index("core")
-    live = live_count(sections)
+    live = counts[:1]
     parts = [
         kept(j < group, jnp.concatenate([got[2 * j], got[2 * j + 1]], 0), R) for j in range(Q - 1)
     ]
@@ -166,7 +168,7 @@
     total = jnp.zeros((F, W), F32)
     pad = jnp.zeros((W - R, W), BF16)
     for t in range(T):
-        state = jnp.where(t < live, states[t, :R] + moved[:, t * W : (t + 1) * W], 0.0)
+        state = jnp.where(float(t) < live, states[t, :R] + moved[:, t * W : (t + 1) * W], 0.0)
         high, low = split(state)
         total += dot(arrow[t], jnp.concatenate([high, pad], 0), (1, 1))
         rows = jnp.concatenate([high, low, arrow[t], jnp.zeros((F, W), BF16)], 0)
@@ -185,13 +187,13 @@
         out[n] = (got[n] + got[K + n]) + (got[2 * K + n] + got[3 * K + n])
 
 
-def arrive_kernel(sections, got, backward, sums, chunk):
-    live = live_count(sections)
+def arrive_kernel(counts, got, backward, sums, chunk):
+    live = counts[:1]
     whole = (got[0] + got[1]) + (got[2] + got[3])
     state = jnp.zeros((G, W), F32)
     for t in reversed(range(T)):
         source = whole[t * G : (t + 1) * G]
-        state = jnp.where(t < live, source - times_t(state, backward[t]), state)
+        state = jnp.where(float(t) < live, source - times_t(state, backward[t]), state)
         sums[t] = state
     chunk[:G] = state
     chunk[G:] = whole[T * G :]
@@ -210,10 +212,22 @@
 
 
 def final_kernel(
-    sections, got, after, after_map, sums, maps, side, tip_inverse, out, tip_out
+    counts,
+    got,
+    after,
+    after_map,
+    sums,
+    maps,
+    side,
+    tip_inverse,
+    out_final,
+    tip_final,
+    out,
+    tip_out,
+    sems,
 ):
     group = lax.axis_index("zg")
-    live = live_count(sections)
+    live = counts[:1]
     whole = got[1, EDGE - F : EDGE]
     for j in range(1, Q):
         whole = whole + got[2 * j + 1, EDGE - F : EDGE]
@@ -225,6 +239,8 @@
         tip_inverse[...], tip, (((0,), (0,)), ((), ())), precision=HI, preferred_element_type=F32
     )
     tip_out[...] = tip
+    copies = [pltpu.make_async_copy(tip_out, tip_final, sems.at[T])]
+    copies[0].start()
 
     parts = []
     for j in reversed(range(1, Q)):
@@ -243,7 +259,11 @@
     fixed = jnp.concatenate([high.astype(F32), high.astype(F32), low.astype(F32)], 0).astype(BF16)
     state = state[:R] - dot(weights, fixed, (0, 0))
     for t in range(T):
-        out[t] = jnp.where(t < live, state[:, t * W : (t + 1) * W], 0.0)
+        out[t] = jnp.where(float(t) < live, state[:, t * W : (t + 1) * W], 0.0)
+        copies.append(pltpu.make_async_copy(out.at[t], out_final.at[t], sems.at[t]))
+        copies[-1].start()
+    for copy in copies:
+        copy.wait()
 
 
 VMEM = pl.BlockSpec(memory_space=pltpu.VMEM)
@@ -251,7 +271,7 @@
 HBM = pl.BlockSpec(memory_space=pltpu.HBM)
 
 
-def call(kernel, shapes, *args, own_copies=False, scratch=()):
+def call(kernel, shapes, *args, own_copies=False, scratch=(), outputs=None):
     specs = [HBM if own_copies else SMEM if a.dtype == jnp.int32 else VMEM for a in args]
     shapes = [s if hasattr(s, "dtype") else jax.ShapeDtypeStruct(s, F32) for s in shapes]
     if own_copies:
@@ -260,7 +280,7 @@
         kernel,
         out_shape=shapes,
         in_specs=specs,
-        out_specs=[VMEM] * len(shapes),
+        out_specs=[outputs or VMEM] * len(shapes),
         scratch_shapes=scratch,
         compiler_params=pltpu.CompilerParams(vmem_limit_bytes=16 << 20),
         name=kernel.__name__,
@@ -280,9 +300,9 @@
     sections, right_side, tip_side, diag_inverse, forward_coupling, backward_coupling, arrow_rows, tip_inverse
 ):
     kept_inputs = [jax.ShapeDtypeStruct(a.shape, BF16) for a in (diag_inverse, backward_coupling)]
-    states, maps, chunk, inverse, backward = call(
+    states, maps, chunk, counts, inverse, backward = call(
         local_kernel,
-        [(T, R + W, W), (T, W, W), (R + 2 * W, W)] + kept_inputs,
+        [(T, R + W, W), (T, W, W), (R + 2 * W, W), (F, W)] + kept_inputs,
         sections,
         right_side,
         diag_inverse,
@@ -304,7 +324,7 @@
     (out,) = call(
         source_kernel,
         [(N, T * G + F, W)],
-        sections,
+        counts,
         got,
         before,
         states,
@@ -314,14 +334,14 @@
     got = lax.all_to_all(out, PLANE, 0, 0, axis_index_groups=along(0), tiled=True)
     (out,) = call(fold_kernel, [(K, T * G + F, W)], got)
     got = lax.all_to_all(out, PLANE, 0, 0, axis_index_groups=along(1), tiled=True)
-    sums, chunk = call(arrive_kernel, [(T, G, W), (G + F, W)], sections, got, backward)
+    sums, chunk = call(arrive_kernel, [(T, G, W), (G + F, W)], counts, got, backward)
     got = lax.all_gather(chunk, NEAR)
     out, after = call(back_group_kernel, [(EDGE + W // 2, W), (G, W)], got, near, back)
     got = lax.all_gather(out, FAR)
     solved, tip = call(
         final_kernel,
         [(T, R, W), (F, R)],
-        sections,
+        counts,
         got,
         after,
         after_map,
@@ -329,6 +349,12 @@
         maps,
         tip_side.T,
         tip_inverse,
+        outputs=HBM,
+        scratch=(
+            pltpu.VMEM((T, R, W), F32),
+            pltpu.VMEM((F, R), F32),
+            pltpu.SemaphoreType.DMA((T + 1,)),
+        ),
     )
     return solved, tip.T
 

time: 111 us -> 109 us (0.982)
  Pallas kernels: 10.2 us -> 8.58 us
    pallas_call x7, Pallas kernels: 10.2 us -> 8.58 us  [call(): pl.pallas_call(kernel, out_shape=shapes, in_specs=specs, out_specs=[outpu...]
where the time goes in v7:
time: 109 us
  blocking collectives  100 us (92%)
  Pallas kernels  8.58 us (8%)
    all_gather x2, blocking collectives, on_device(): got = lax.all_gather(out, FAR)  45.8 us
    all_to_all x1, blocking collectives, on_device(): lax.all_to_all(out, PLANE, 0, 0, axis_index_groups=along(0), tiled=True)  21.1 us
    all_gather x1, blocking collectives, on_device(): near = lax.all_gather(chunk, NEAR)  13.5 us
    all_to_all x1, blocking collectives, on_device(): lax.all_to_all(out, PLANE, 0, 0, axis_index_groups=along(1), tiled=True)  11.3 us
    pallas_call x7, Pallas kernels, call(): pl.pallas_call(kernel, out_shape=shapes, in_specs=specs, out_specs=[outpu...  8.58 us
    all_gather x1, blocking collectives, on_device(): got = lax.all_gather(chunk, NEAR)  8.28 us

profile of v7, /device:TPU:1, one launch (start us, length us, event | category | flops | bytes accessed | tf_op | source)
XLA Modules:
  0.0 109.3 jit_solution(1618164083294646221)
XLA Ops:
  0.6 0.0 copy-start
  0.6 3.6 %local_kernel.1 = (f32[4,192,128]{2,1,0:T(8,128)S(1)}, f32[4,128,128]{2,1,0:T(8,128)S(1)}, f32[320,128]{1,0:T(8,128)S(1)}, f32[8,128]{1,0:T(8,128)S(1)}, bf16[4,...) custom-call(s32[32]{0:T(128)} %sections_in.1, bf16[4,64,2048]{2,1,0:T(8,128)(2,1)} %side_in.1, ...), custom_call_target="tpu_custom_call" | custom-call | tf_op jit(solution)/shard_map/local_kernel/pallas_call | solution.py:279
  4.2 13.5 %all-gather = f32[1280,128]{1,0:T(8,128)S(1)} all-gather(f32[320,128]{1,0:T(8,128)S(1)} %get-tuple-element.19), channel_id=2, replica_groups=mesh['zg'=8,'zp'=2,'core'=2,'x'=4,'y'=4] {'zp','core'}, dimensions={0}, use_global_device_ids=true | all-gather | bytes 819200 | tf_op jit(solution)/shard_map/all_gather | solution.py:319
  17.8 0.5 group_kernel.1
  18.2 24.8 %all-gather.1 = f32[1536,128]{1,0:T(8,128)S(1)} all-gather(f32[96,128]{1,0:T(8,128)S(1)} %get-tuple-element.20), channel_id=3, replica_groups=mesh['zg'=8,'zp'=2,'core'=2,'x'=4,'y'=4] {'zg','core'}, dimensions={0}, use_global_device_ids=true | all-gather | bytes 835584 | tf_op jit(solution)/shard_map/all_gather | solution.py:323
  43.1 0.0 copy-done
  43.1 1.6 %source_kernel.1 = f32[16,296,128]{2,1,0:T(8,128)S(1)} custom-call(f32[8,128]{1,0:T(8,128)S(1)} %get-tuple-element.18.counts, f32[16,96,128]{2,1,0:T(8,128)S(1)} %bitcast.9, f32[192,128]{1,0:T(8,128)S(1)} %get-tuple-element.21.before, f32[4,192,128]{2,1,0:T(8,128)S(1)} %get-tuple-element.22.states, bf16[4,128,2048]{2,1,0:T(8,128)(2,1)S(1)} %get-tuple-element.23.inverse, ...), custom_call_target="tpu_custom_call" | custom-call | tf_op jit(solution)/shard_map/source_kernel/pallas_call | solution.py:279
  44.7 21.1 %all_to_all.10.got = f32[16,296,128]{2,1,0:T(8,128)S(1)} all-to-all(f32[16,296,128]{2,1,0:T(8,128)S(1)} %source_kernel.1), channel_id=1, replica_groups={{0,4,8,12},{1,5,9,13},{2,6,10,14},{3,7,11,15},{16,17,18,19},{20,21,22,2..., dimensions={0} | all-to-all | bytes 4849664 | tf_op jit(solution)/shard_map/all_to_all | solution.py:334
  65.8 0.1 fold_kernel.1
  65.9 0.0 copy-start.1
  65.9 0.0 copy-start.2
  65.9 11.3 %all_to_all.11.got = f32[4,296,128]{2,1,0:T(8,128)S(1)} all-to-all(f32[4,296,128]{2,1,0:T(8,128)S(1)} %fold_kernel.1), channel_id=1, replica_groups={{0,1,2,3},{4,5,6,7},{8,9,10,11},{12,13,14,15},{16,20,24,28},{17,21,25,2..., dimensions={0} | all-to-all | bytes 1212416 | tf_op jit(solution)/shard_map/all_to_all | solution.py:336
  77.2 0.5 arrive_kernel.1
  77.7 8.3 %all-gather.2 = f32[320,128]{1,0:T(8,128)S(1)} all-gather(f32[80,128]{1,0:T(8,128)S(1)} %get-tuple-element.25), channel_id=4, replica_groups=mesh['zg'=8,'zp'=2,'core'=2,'x'=4,'y'=4] {'zp','core'}, dimensions={0}, use_global_device_ids=true | all-gather | bytes 204800 | tf_op jit(solution)/shard_map/all_gather | solution.py:338
  86.0 0.4 back_group_kernel.1
  86.4 21.0 %all-gather.3 = f32[1664,128]{1,0:T(8,128)S(1)} all-gather(f32[104,128]{1,0:T(8,128)S(1)} %get-tuple-element.27), channel_id=5, replica_groups=mesh['zg'=8,'zp'=2,'core'=2,'x'=4,'y'=4] {'zg','core'}, dimensions={0}, use_global_device_ids=true | all-gather | bytes 905216 | tf_op jit(solution)/shard_map/all_gather | solution.py:340
  107.4 0.0 copy-done.1
  107.4 0.0 copy-done.2
  107.4 1.9 %final_kernel.1 = (f32[4,64,128]{2,1,0:T(8,128)}, f32[8,64]{1,0:T(8,128)}) custom-call(f32[8,128]{1,0:T(8,128)S(1)} %get-tuple-element.18.counts, f32[16,104,128]{2,1,0:T(8,128)S(1)} %bitcast.8, f32[72,128]{1,0:T(8,128)S(1)} %get-tuple-element.28.after, f32[128,128]{1,0:T(8,128)S(1)} %get-tuple-element.29.after_map, ...), custom_call_target="tpu_custom_call" | custom-call | tf_op jit(solution)/shard_map/final_kernel/pallas_call | solution.py:279
Async XLA Ops:
  0.6 42.4 %copy-start = (bf16[4,8,128]{2,1,0:T(8,128)(2,1)S(1)}, bf16[4,8,128]{2,1,0:T(8,128)(2,1)}, u32[]{:S(2)}) copy-start(bf16[4,8,128]{2,1,0:T(8,128)(2,1)} %arrow.1) | copy-start | bytes 24580
  65.9 41.5 %copy-start.1 = (f32[64,8]{0,1:T(8,128)S(1)}, f32[64,8]{0,1:T(8,128)}, u32[]{:S(2)}) copy-start(f32[64,8]{0,1:T(8,128)} %param.10) | copy-start | bytes 6148
  65.9 41.5 %copy-start.2 = (f32[8,8]{1,0:T(8,128)S(1)}, f32[8,8]{1,0:T(8,128)}, u32[]{:S(2)}) copy-start(f32[8,8]{1,0:T(8,128)} %tip_inverse.1) | copy-start | bytes 772

commit v8 on v7

--- a/solution.py
+++ b/solution.py
@@ -127,15 +127,15 @@
             mapping = jnp.where(t < live, -times_t(mapping, forward[t]), mapping)
         states[t, R:] = mapping
     chunk[R : R + W] = mapping
-    state = None
-    for t in range(T):
-        copies[3 + 2 * t].wait()
-        copies[4 + 2 * t].wait()
-        driven = dot(side[t], inverse[t], (1, 1))
-        if t == 0:
-            state = driven
-        else:
-            state = jnp.where(t < live, driven - times_t(state, forward[t]), state)
+    driven = []
+    for first in (0, 2):
+        for copy in copies[3 + 2 * first : 7 + 2 * first]:
+            copy.wait()
+        driven += [dot(side[t], inverse[t], (1, 1)) for t in (first, first + 1)]
+    state = driven[0]
+    states[0, :R] = state
+    for t in range(1, T):
+        state = jnp.where(t < live, driven[t] - times_t(state, forward[t]), state)
         states[t, :R] = state
     chunk[:R] = state
 

time: 109 us -> 109 us (level)
  no operation moved by 1% of the time
where the time goes in v8:
time: 109 us
  blocking collectives  100 us (92%)
  Pallas kernels  8.18 us (8%)
    all_gather x2, blocking collectives, on_device(): got = lax.all_gather(out, FAR)  45.8 us
    all_to_all x1, blocking collectives, on_device(): lax.all_to_all(out, PLANE, 0, 0, axis_index_groups=along(0), tiled=True)  21.1 us
    all_gather x1, blocking collectives, on_device(): near = lax.all_gather(chunk, NEAR)  13.5 us
    all_to_all x1, blocking collectives, on_device(): lax.all_to_all(out, PLANE, 0, 0, axis_index_groups=along(1), tiled=True)  11.3 us
    all_gather x1, blocking collectives, on_device(): got = lax.all_gather(chunk, NEAR)  8.28 us
    pallas_call x7, Pallas kernels, call(): pl.pallas_call(kernel, out_shape=shapes, in_specs=specs, out_specs=[outpu...  8.18 us

profile of v8, /device:TPU:1, one launch (start us, length us, event | category | flops | bytes accessed | tf_op | source)
XLA Modules:
  0.0 108.9 jit_solution(12573197023459858434)
XLA Ops:
  0.6 0.0 copy-start
  0.6 3.2 %local_kernel.1 = (f32[4,192,128]{2,1,0:T(8,128)S(1)}, f32[4,128,128]{2,1,0:T(8,128)S(1)}, f32[320,128]{1,0:T(8,128)S(1)}, f32[8,128]{1,0:T(8,128)S(1)}, bf16[4,...) custom-call(s32[32]{0:T(128)} %sections_in.1, bf16[4,64,2048]{2,1,0:T(8,128)(2,1)} %side_in.1, ...), custom_call_target="tpu_custom_call" | custom-call | tf_op jit(solution)/shard_map/local_kernel/pallas_call | solution.py:279
  3.8 13.5 %all-gather = f32[1280,128]{1,0:T(8,128)S(1)} all-gather(f32[320,128]{1,0:T(8,128)S(1)} %get-tuple-element.19), channel_id=2, replica_groups=mesh['zg'=8,'zp'=2,'core'=2,'x'=4,'y'=4] {'zp','core'}, dimensions={0}, use_global_device_ids=true | all-gather | bytes 819200 | tf_op jit(solution)/shard_map/all_gather | solution.py:319
  17.4 0.5 group_kernel.1
  17.8 24.8 %all-gather.1 = f32[1536,128]{1,0:T(8,128)S(1)} all-gather(f32[96,128]{1,0:T(8,128)S(1)} %get-tuple-element.20), channel_id=3, replica_groups=mesh['zg'=8,'zp'=2,'core'=2,'x'=4,'y'=4] {'zg','core'}, dimensions={0}, use_global_device_ids=true | all-gather | bytes 835584 | tf_op jit(solution)/shard_map/all_gather | solution.py:323
  42.7 0.0 copy-done
  42.7 1.6 %source_kernel.1 = f32[16,296,128]{2,1,0:T(8,128)S(1)} custom-call(f32[8,128]{1,0:T(8,128)S(1)} %get-tuple-element.18.counts, f32[16,96,128]{2,1,0:T(8,128)S(1)} %bitcast.9, f32[192,128]{1,0:T(8,128)S(1)} %get-tuple-element.21.before, f32[4,192,128]{2,1,0:T(8,128)S(1)} %get-tuple-element.22.states, bf16[4,128,2048]{2,1,0:T(8,128)(2,1)S(1)} %get-tuple-element.23.inverse, ...), custom_call_target="tpu_custom_call" | custom-call | tf_op jit(solution)/shard_map/source_kernel/pallas_call | solution.py:279
  44.3 21.1 %all_to_all.10.got = f32[16,296,128]{2,1,0:T(8,128)S(1)} all-to-all(f32[16,296,128]{2,1,0:T(8,128)S(1)} %source_kernel.1), channel_id=1, replica_groups={{0,4,8,12},{1,5,9,13},{2,6,10,14},{3,7,11,15},{16,17,18,19},{20,21,22,2..., dimensions={0} | all-to-all | bytes 4849664 | tf_op jit(solution)/shard_map/all_to_all | solution.py:334
  65.4 0.1 fold_kernel.1
  65.5 0.0 copy-start.1
  65.5 0.0 copy-start.2
  65.5 11.3 %all_to_all.11.got = f32[4,296,128]{2,1,0:T(8,128)S(1)} all-to-all(f32[4,296,128]{2,1,0:T(8,128)S(1)} %fold_kernel.1), channel_id=1, replica_groups={{0,1,2,3},{4,5,6,7},{8,9,10,11},{12,13,14,15},{16,20,24,28},{17,21,25,2..., dimensions={0} | all-to-all | bytes 1212416 | tf_op jit(solution)/shard_map/all_to_all | solution.py:336
  76.8 0.5 arrive_kernel.1
  77.3 8.3 %all-gather.2 = f32[320,128]{1,0:T(8,128)S(1)} all-gather(f32[80,128]{1,0:T(8,128)S(1)} %get-tuple-element.25), channel_id=4, replica_groups=mesh['zg'=8,'zp'=2,'core'=2,'x'=4,'y'=4] {'zp','core'}, dimensions={0}, use_global_device_ids=true | all-gather | bytes 204800 | tf_op jit(solution)/shard_map/all_gather | solution.py:338
  85.6 0.4 back_group_kernel.1
  86.0 21.0 %all-gather.3 = f32[1664,128]{1,0:T(8,128)S(1)} all-gather(f32[104,128]{1,0:T(8,128)S(1)} %get-tuple-element.27), channel_id=5, replica_groups=mesh['zg'=8,'zp'=2,'core'=2,'x'=4,'y'=4] {'zg','core'}, dimensions={0}, use_global_device_ids=true | all-gather | bytes 905216 | tf_op jit(solution)/shard_map/all_gather | solution.py:340
  107.0 0.0 copy-done.1
  107.0 0.0 copy-done.2
  107.0 1.9 %final_kernel.1 = (f32[4,64,128]{2,1,0:T(8,128)}, f32[8,64]{1,0:T(8,128)}) custom-call(f32[8,128]{1,0:T(8,128)S(1)} %get-tuple-element.18.counts, f32[16,104,128]{2,1,0:T(8,128)S(1)} %bitcast.8, f32[72,128]{1,0:T(8,128)S(1)} %get-tuple-element.28.after, f32[128,128]{1,0:T(8,128)S(1)} %get-tuple-element.29.after_map, ...), custom_call_target="tpu_custom_call" | custom-call | tf_op jit(solution)/shard_map/final_kernel/pallas_call | solution.py:279
Async XLA Ops:
  0.6 42.0 %copy-start = (bf16[4,8,128]{2,1,0:T(8,128)(2,1)S(1)}, bf16[4,8,128]{2,1,0:T(8,128)(2,1)}, u32[]{:S(2)}) copy-start(bf16[4,8,128]{2,1,0:T(8,128)(2,1)} %arrow.1) | copy-start | bytes 24580
  65.5 41.5 %copy-start.1 = (f32[64,8]{0,1:T(8,128)S(1)}, f32[64,8]{0,1:T(8,128)}, u32[]{:S(2)}) copy-start(f32[64,8]{0,1:T(8,128)} %param.10) | copy-start | bytes 6148
  65.5 41.5 %copy-start.2 = (f32[8,8]{1,0:T(8,128)S(1)}, f32[8,8]{1,0:T(8,128)}, u32[]{:S(2)}) copy-start(f32[8,8]{1,0:T(8,128)} %tip_inverse.1) | copy-start | bytes 772

commit v9 on v8

--- a/solution.py
+++ b/solution.py
@@ -62,22 +62,23 @@
     return sections[lax.axis_index("zg") * L + near_index()]
 
 
-def join(first, then, rows=R):
-    out = times(first, then[rows:])
-    return jnp.concatenate([out[:rows] + then[:rows], out[rows:]], 0)
-
-
-def offset_of(parts, rows):
-    ahead = times(parts[0][:rows], parts[1][rows:]) + parts[1][:rows]
-    middle = join(parts[2], parts[3], rows)
-    behind = join(join(parts[4], parts[5], rows), parts[6], rows)
-    ahead = times(ahead, middle[rows:]) + middle[:rows]
-    return times(ahead, behind[rows:]) + behind[:rows]
-
-
-def kept(flag, part, rows):
-    neutral = jnp.concatenate([jnp.zeros((rows, W), F32), eye(F32)], 0)
-    return jnp.where(flag, part, neutral)
+def times_tall(x, m):
+    xh, xl = split(x)
+    mh, ml = split(m)
+    both = dot(jnp.concatenate([xh, xl], 0), mh, (1, 0))
+    return both[: x.shape[0]] + both[x.shape[0] :] + dot(xh, ml, (1, 0))
+
+
+def join(first, then):
+    out = times_tall(first, then[R:])
+    return jnp.concatenate([out[:R] + then[:R], out[R:]], 0)
+
+
+def offset_of(parts, flags):
+    ahead = jnp.where(flags[0], parts[0][0], 0.0)
+    for flag, (offset, mapping) in zip(flags[1:], parts[1:]):
+        ahead = jnp.where(flag, times(ahead, mapping) + offset, ahead)
+    return ahead
 
 
 def half_of(x):
@@ -150,7 +151,7 @@
         before[...] = jnp.where(me == j, total, before[...])
         total = join(total, got[j, : R + W])
         after[...] = jnp.where(me == L - 1 - j, mapping, after[...])
-        mapping = times(mapping, got[L - 1 - j, R + W :])
+        mapping = times_tall(mapping, got[L - 1 - j, R + W :])
     out[...] = half_of(total)
     back[...] = half_of(mapping)
 
@@ -160,9 +161,9 @@
     core = lax.axis_index("core")
     live = counts[:1]
     parts = [
-        kept(j < group, jnp.concatenate([got[2 * j], got[2 * j + 1]], 0), R) for j in range(Q - 1)
+        (got[2 * j, :R], jnp.concatenate([got[2 * j, R:], got[2 * j + 1]], 0)) for j in range(Q - 1)
     ]
-    entry = offset_of(parts, R)
+    entry = offset_of(parts, [j < group for j in range(Q - 1)])
     entry = times(entry, before[R:]) + before[:R]
     moved = times(entry, jnp.concatenate([states[t, R:] for t in range(T)], 1))
     total = jnp.zeros((F, W), F32)
@@ -245,9 +246,9 @@
     parts = []
     for j in reversed(range(1, Q)):
         first, second = got[2 * j], got[2 * j + 1]
-        part = [first[:EDGE], second[: EDGE - F], first[EDGE:], second[EDGE:]]
-        parts.append(kept(j > group, jnp.concatenate(part, 0), G))
-    entry = offset_of(parts, G)
+        offset = jnp.concatenate([first[:EDGE], second[: EDGE - F]], 0)
+        parts.append((offset, jnp.concatenate([first[EDGE:], second[EDGE:]], 0)))
+    entry = offset_of(parts, [j > group for j in reversed(range(1, Q))])
     entry = times(entry, after_map[...]) + after[...]
     state = times(entry, jnp.concatenate([maps[t] for t in range(T)], 1))
     state = state + jnp.concatenate([sums[t] for t in range(T)], 1)

time: 109 us -> 110 us (level)
  no operation moved by 1% of the time
where the time goes in v9:
time: 110 us
  blocking collectives  100 us (91%)
  Pallas kernels  8.7 us (8%)
    all_gather x2, blocking collectives, on_device(): got = lax.all_gather(out, FAR)  46 us
    all_to_all x1, blocking collectives, on_device(): lax.all_to_all(out, PLANE, 0, 0, axis_index_groups=along(0), tiled=True)  20.9 us
    all_gather x1, blocking collectives, on_device(): near = lax.all_gather(chunk, NEAR)  13.5 us
    all_to_all x1, blocking collectives, on_device(): lax.all_to_all(out, PLANE, 0, 0, axis_index_groups=along(1), tiled=True)  11.4 us
    pallas_call x7, Pallas kernels, call(): pl.pallas_call(kernel, out_shape=shapes, in_specs=specs, out_specs=[outpu...  8.7 us
    all_gather x1, blocking collectives, on_device(): got = lax.all_gather(chunk, NEAR)  8.28 us

profile of v9, /device:TPU:1, one launch (start us, length us, event | category | flops | bytes accessed | tf_op | source)
XLA Modules:
  0.0 109.6 jit_solution(3971334398403896036)
XLA Ops:
  0.6 0.0 copy-start
  0.6 3.2 %local_kernel.1 = (f32[4,192,128]{2,1,0:T(8,128)S(1)}, f32[4,128,128]{2,1,0:T(8,128)S(1)}, f32[320,128]{1,0:T(8,128)S(1)}, f32[8,128]{1,0:T(8,128)S(1)}, bf16[4,...) custom-call(s32[32]{0:T(128)} %sections_in.1, bf16[4,64,2048]{2,1,0:T(8,128)(2,1)} %side_in.1, ...), custom_call_target="tpu_custom_call" | custom-call | tf_op jit(solution)/shard_map/local_kernel/pallas_call | solution.py:280
  3.8 13.5 %all-gather = f32[1280,128]{1,0:T(8,128)S(1)} all-gather(f32[320,128]{1,0:T(8,128)S(1)} %get-tuple-element.19), channel_id=2, replica_groups=mesh['zg'=8,'zp'=2,'core'=2,'x'=4,'y'=4] {'zp','core'}, dimensions={0}, use_global_device_ids=true | all-gather | bytes 819200 | tf_op jit(solution)/shard_map/all_gather | solution.py:320
  17.4 0.6 group_kernel.1
  17.9 24.8 %all-gather.1 = f32[1536,128]{1,0:T(8,128)S(1)} all-gather(f32[96,128]{1,0:T(8,128)S(1)} %get-tuple-element.20), channel_id=3, replica_groups=mesh['zg'=8,'zp'=2,'core'=2,'x'=4,'y'=4] {'zg','core'}, dimensions={0}, use_global_device_ids=true | all-gather | bytes 835584 | tf_op jit(solution)/shard_map/all_gather | solution.py:324
  42.8 0.0 copy-done
  42.8 1.8 %source_kernel.1 = f32[16,296,128]{2,1,0:T(8,128)S(1)} custom-call(f32[8,128]{1,0:T(8,128)S(1)} %get-tuple-element.18.counts, f32[16,96,128]{2,1,0:T(8,128)S(1)} %bitcast.9, f32[192,128]{1,0:T(8,128)S(1)} %get-tuple-element.21.before, f32[4,192,128]{2,1,0:T(8,128)S(1)} %get-tuple-element.22.states, bf16[4,128,2048]{2,1,0:T(8,128)(2,1)S(1)} %get-tuple-element.23.inverse, ...), custom_call_target="tpu_custom_call" | custom-call | tf_op jit(solution)/shard_map/source_kernel/pallas_call | solution.py:280
  44.6 20.9 %all_to_all.10.got = f32[16,296,128]{2,1,0:T(8,128)S(1)} all-to-all(f32[16,296,128]{2,1,0:T(8,128)S(1)} %source_kernel.1), channel_id=1, replica_groups={{0,4,8,12},{1,5,9,13},{2,6,10,14},{3,7,11,15},{16,17,18,19},{20,21,22,2..., dimensions={0} | all-to-all | bytes 4849664 | tf_op jit(solution)/shard_map/all_to_all | solution.py:335
  65.5 0.1 fold_kernel.1
  65.7 0.0 copy-start.1
  65.7 0.0 copy-start.2
  65.7 11.4 %all_to_all.11.got = f32[4,296,128]{2,1,0:T(8,128)S(1)} all-to-all(f32[4,296,128]{2,1,0:T(8,128)S(1)} %fold_kernel.1), channel_id=1, replica_groups={{0,1,2,3},{4,5,6,7},{8,9,10,11},{12,13,14,15},{16,20,24,28},{17,21,25,2..., dimensions={0} | all-to-all | bytes 1212416 | tf_op jit(solution)/shard_map/all_to_all | solution.py:337
  77.1 0.5 arrive_kernel.1
  77.6 8.3 %all-gather.2 = f32[320,128]{1,0:T(8,128)S(1)} all-gather(f32[80,128]{1,0:T(8,128)S(1)} %get-tuple-element.25), channel_id=4, replica_groups=mesh['zg'=8,'zp'=2,'core'=2,'x'=4,'y'=4] {'zp','core'}, dimensions={0}, use_global_device_ids=true | all-gather | bytes 204800 | tf_op jit(solution)/shard_map/all_gather | solution.py:339
  85.9 0.4 back_group_kernel.1
  86.3 21.1 %all-gather.3 = f32[1664,128]{1,0:T(8,128)S(1)} all-gather(f32[104,128]{1,0:T(8,128)S(1)} %get-tuple-element.27), channel_id=5, replica_groups=mesh['zg'=8,'zp'=2,'core'=2,'x'=4,'y'=4] {'zg','core'}, dimensions={0}, use_global_device_ids=true | all-gather | bytes 905216 | tf_op jit(solution)/shard_map/all_gather | solution.py:341
  107.5 0.0 copy-done.1
  107.5 0.0 copy-done.2
  107.5 2.1 %final_kernel.1 = (f32[4,64,128]{2,1,0:T(8,128)}, f32[8,64]{1,0:T(8,128)}) custom-call(f32[8,128]{1,0:T(8,128)S(1)} %get-tuple-element.18.counts, f32[16,104,128]{2,1,0:T(8,128)S(1)} %bitcast.8, f32[72,128]{1,0:T(8,128)S(1)} %get-tuple-element.28.after, f32[128,128]{1,0:T(8,128)S(1)} %get-tuple-element.29.after_map, ...), custom_call_target="tpu_custom_call" | custom-call | tf_op jit(solution)/shard_map/final_kernel/pallas_call | solution.py:280
Async XLA Ops:
  0.6 42.1 %copy-start = (bf16[4,8,128]{2,1,0:T(8,128)(2,1)S(1)}, bf16[4,8,128]{2,1,0:T(8,128)(2,1)}, u32[]{:S(2)}) copy-start(bf16[4,8,128]{2,1,0:T(8,128)(2,1)} %arrow.1) | copy-start | bytes 24580
  65.7 41.8 %copy-start.1 = (f32[64,8]{0,1:T(8,128)S(1)}, f32[64,8]{0,1:T(8,128)}, u32[]{:S(2)}) copy-start(f32[64,8]{0,1:T(8,128)} %param.10) | copy-start | bytes 6148
  65.7 41.8 %copy-start.2 = (f32[8,8]{1,0:T(8,128)S(1)}, f32[8,8]{1,0:T(8,128)}, u32[]{:S(2)}) copy-start(f32[8,8]{1,0:T(8,128)} %tip_inverse.1) | copy-start | bytes 772

commit v10 on v8

--- a/solution.py
+++ b/solution.py
@@ -70,7 +70,7 @@
 def offset_of(parts, rows):
     ahead = times(parts[0][:rows], parts[1][rows:]) + parts[1][:rows]
     middle = join(parts[2], parts[3], rows)
-    behind = join(join(parts[4], parts[5], rows), parts[6], rows)
+    behind = join(join(parts[4], parts[5], rows), join(parts[6], parts[7], rows), rows)
     ahead = times(ahead, middle[rows:]) + middle[:rows]
     return times(ahead, behind[rows:]) + behind[:rows]
 
@@ -140,19 +140,24 @@
     chunk[:R] = state
 
 
+def picked(choices):
+    me = near_index()
+    out = choices[0]
+    for j in range(1, L):
+        out = jnp.where(me == j, choices[j], out)
+    return out
+
+
 def group_kernel(got, out, back, before, after):
-    me = near_index()
-    total = got[0, : R + W]
-    before[...] = jnp.concatenate([jnp.zeros((R, W), F32), eye(F32)], 0)
-    mapping = got[L - 1, R + W :]
-    after[...] = eye(F32)
-    for j in range(1, L):
-        before[...] = jnp.where(me == j, total, before[...])
-        total = join(total, got[j, : R + W])
-        after[...] = jnp.where(me == L - 1 - j, mapping, after[...])
-        mapping = times(mapping, got[L - 1 - j, R + W :])
-    out[...] = half_of(total)
-    back[...] = half_of(mapping)
+    parts = [got[j, : R + W] for j in range(L)]
+    maps = [got[j, R + W :] for j in range(L)]
+    first, second = join(parts[0], parts[1]), join(parts[2], parts[3])
+    late, early = times(maps[3], maps[2]), times(maps[1], maps[0])
+    neutral = jnp.concatenate([jnp.zeros((R, W), F32), eye(F32)], 0)
+    before[...] = picked([neutral, parts[0], first, join(first, parts[2])])
+    after[...] = picked([times(late, maps[1]), late, maps[3], eye(F32)])
+    out[...] = half_of(join(first, second))
+    back[...] = half_of(times(late, early))
 
 
 def source_kernel(counts, got, before, states, inverse, arrow, out):
@@ -162,8 +167,7 @@
     parts = [
         kept(j < group, jnp.concatenate([got[2 * j], got[2 * j + 1]], 0), R) for j in range(Q - 1)
     ]
-    entry = offset_of(parts, R)
-    entry = times(entry, before[R:]) + before[:R]
+    entry = offset_of(parts + [before[...]], R)
     moved = times(entry, jnp.concatenate([states[t, R:] for t in range(T)], 1))
     total = jnp.zeros((F, W), F32)
     pad = jnp.zeros((W - R, W), BF16)
@@ -200,12 +204,12 @@
 
 
 def back_group_kernel(got, maps, mapping, out, after):
-    me = near_index()
-    total = got[L - 1, :G]
-    after[...] = jnp.zeros((G, W), F32)
-    for j in reversed(range(L - 1)):
-        after[...] = jnp.where(me == j, total, after[...])
-        total = times(total, maps[j, R + W :]) + got[j, :G]
+    parts = [got[j, :G] for j in range(L)]
+    steps = [maps[j, R + W :] for j in range(L)]
+    late = times(parts[3], steps[2]) + parts[2]
+    early = times(parts[1], steps[0]) + parts[0]
+    total = times(late, times(steps[1], steps[0])) + early
+    after[...] = picked([times(late, steps[1]) + parts[1], late, parts[3], jnp.zeros((G, W), F32)])
     whole = ((got[0, G:] + got[1, G:]) + got[2, G:]) + got[3, G:]
     out[:EDGE] = half_of(jnp.concatenate([total, whole], 0))
     out[EDGE:] = mapping[...]
@@ -247,8 +251,8 @@
         first, second = got[2 * j], got[2 * j + 1]
         part = [first[:EDGE], second[: EDGE - F], first[EDGE:], second[EDGE:]]
         parts.append(kept(j > group, jnp.concatenate(part, 0), G))
+    parts.append(jnp.concatenate([after[...], after_map[...]], 0))
     entry = offset_of(parts, G)
-    entry = times(entry, after_map[...]) + after[...]
     state = times(entry, jnp.concatenate([maps[t] for t in range(T)], 1))
     state = state + jnp.concatenate([sums[t] for t in range(T)], 1)
     tip_high, tip_low = split(tip)

time: 109 us -> 109 us (level)
  no operation moved by 1% of the time
where the time goes in v10:
time: 109 us; the launch traced here: 108 us
  blocking collectives  99.6 us (91%)
  Pallas kernels  8.13 us (7%)
    all_gather x2, blocking collectives, on_device(): got = lax.all_gather(out, FAR)  45.4 us
    all_to_all x1, blocking collectives, on_device(): lax.all_to_all(out, PLANE, 0, 0, axis_index_groups=along(0), tiled=True)  21.1 us
    all_gather x1, blocking collectives, on_device(): near = lax.all_gather(chunk, NEAR)  13.5 us
    all_to_all x1, blocking collectives, on_device(): lax.all_to_all(out, PLANE, 0, 0, axis_index_groups=along(1), tiled=True)  11.3 us
    all_gather x1, blocking collectives, on_device(): got = lax.all_gather(chunk, NEAR)  8.28 us
    pallas_call x7, Pallas kernels, call(): pl.pallas_call(kernel, out_shape=shapes, in_specs=specs, out_specs=[outpu...  8.13 us

profile of v10, /device:TPU:1, one launch (start us, length us, event | category | flops | bytes accessed | tf_op | source)
XLA Modules:
  0.0 108.4 jit_solution(17528861999815448536)
XLA Ops:
  0.6 0.0 copy-start
  0.6 3.2 %local_kernel.1 = (f32[4,192,128]{2,1,0:T(8,128)S(1)}, f32[4,128,128]{2,1,0:T(8,128)S(1)}, f32[320,128]{1,0:T(8,128)S(1)}, f32[8,128]{1,0:T(8,128)S(1)}, bf16[4,...) custom-call(s32[32]{0:T(128)} %sections_in.1, bf16[4,64,2048]{2,1,0:T(8,128)(2,1)} %side_in.1, ...), custom_call_target="tpu_custom_call" | custom-call | tf_op jit(solution)/shard_map/local_kernel/pallas_call | solution.py:283
  3.8 13.5 %all-gather = f32[1280,128]{1,0:T(8,128)S(1)} all-gather(f32[320,128]{1,0:T(8,128)S(1)} %get-tuple-element.19), channel_id=2, replica_groups=mesh['zg'=8,'zp'=2,'core'=2,'x'=4,'y'=4] {'zp','core'}, dimensions={0}, use_global_device_ids=true | all-gather | bytes 819200 | tf_op jit(solution)/shard_map/all_gather | solution.py:323
  17.4 0.5 group_kernel.1
  17.8 24.8 %all-gather.1 = f32[1536,128]{1,0:T(8,128)S(1)} all-gather(f32[96,128]{1,0:T(8,128)S(1)} %get-tuple-element.20), channel_id=3, replica_groups=mesh['zg'=8,'zp'=2,'core'=2,'x'=4,'y'=4] {'zg','core'}, dimensions={0}, use_global_device_ids=true | all-gather | bytes 835584 | tf_op jit(solution)/shard_map/all_gather | solution.py:327
  42.7 0.0 copy-done
  42.7 1.6 %source_kernel.1 = f32[16,296,128]{2,1,0:T(8,128)S(1)} custom-call(f32[8,128]{1,0:T(8,128)S(1)} %get-tuple-element.18.counts, f32[16,96,128]{2,1,0:T(8,128)S(1)} %bitcast.9, f32[192,128]{1,0:T(8,128)S(1)} %get-tuple-element.21.before, f32[4,192,128]{2,1,0:T(8,128)S(1)} %get-tuple-element.22.states, bf16[4,128,2048]{2,1,0:T(8,128)(2,1)S(1)} %get-tuple-element.23.inverse, ...), custom_call_target="tpu_custom_call" | custom-call | tf_op jit(solution)/shard_map/source_kernel/pallas_call | solution.py:283
  44.3 21.1 %all_to_all.10.got = f32[16,296,128]{2,1,0:T(8,128)S(1)} all-to-all(f32[16,296,128]{2,1,0:T(8,128)S(1)} %source_kernel.1), channel_id=1, replica_groups={{0,4,8,12},{1,5,9,13},{2,6,10,14},{3,7,11,15},{16,17,18,19},{20,21,22,2..., dimensions={0} | all-to-all | bytes 4849664 | tf_op jit(solution)/shard_map/all_to_all | solution.py:338
  65.4 0.1 fold_kernel.1
  65.5 0.0 copy-start.1
  65.5 0.0 copy-start.2
  65.5 11.3 %all_to_all.11.got = f32[4,296,128]{2,1,0:T(8,128)S(1)} all-to-all(f32[4,296,128]{2,1,0:T(8,128)S(1)} %fold_kernel.1), channel_id=1, replica_groups={{0,1,2,3},{4,5,6,7},{8,9,10,11},{12,13,14,15},{16,20,24,28},{17,21,25,2..., dimensions={0} | all-to-all | bytes 1212416 | tf_op jit(solution)/shard_map/all_to_all | solution.py:340
  76.8 0.5 arrive_kernel.1
  77.3 8.3 %all-gather.2 = f32[320,128]{1,0:T(8,128)S(1)} all-gather(f32[80,128]{1,0:T(8,128)S(1)} %get-tuple-element.25), channel_id=4, replica_groups=mesh['zg'=8,'zp'=2,'core'=2,'x'=4,'y'=4] {'zp','core'}, dimensions={0}, use_global_device_ids=true | all-gather | bytes 204800 | tf_op jit(solution)/shard_map/all_gather | solution.py:342
  85.6 0.4 back_group_kernel.1
  86.0 20.6 %all-gather.3 = f32[1664,128]{1,0:T(8,128)S(1)} all-gather(f32[104,128]{1,0:T(8,128)S(1)} %get-tuple-element.27), channel_id=5, replica_groups=mesh['zg'=8,'zp'=2,'core'=2,'x'=4,'y'=4] {'zg','core'}, dimensions={0}, use_global_device_ids=true | all-gather | bytes 905216 | tf_op jit(solution)/shard_map/all_gather | solution.py:344
  106.6 0.0 copy-done.1
  106.6 0.0 copy-done.2
  106.6 1.8 %final_kernel.1 = (f32[4,64,128]{2,1,0:T(8,128)}, f32[8,64]{1,0:T(8,128)}) custom-call(f32[8,128]{1,0:T(8,128)S(1)} %get-tuple-element.18.counts, f32[16,104,128]{2,1,0:T(8,128)S(1)} %bitcast.8, f32[72,128]{1,0:T(8,128)S(1)} %get-tuple-element.28.after, f32[128,128]{1,0:T(8,128)S(1)} %get-tuple-element.29.after_map, ...), custom_call_target="tpu_custom_call" | custom-call | tf_op jit(solution)/shard_map/final_kernel/pallas_call | solution.py:283
Async XLA Ops:
  0.6 42.0 %copy-start = (bf16[4,8,128]{2,1,0:T(8,128)(2,1)S(1)}, bf16[4,8,128]{2,1,0:T(8,128)(2,1)}, u32[]{:S(2)}) copy-start(bf16[4,8,128]{2,1,0:T(8,128)(2,1)} %arrow.1) | copy-start | bytes 24580
  65.5 41.1 %copy-start.1 = (f32[64,8]{0,1:T(8,128)S(1)}, f32[64,8]{0,1:T(8,128)}, u32[]{:S(2)}) copy-start(f32[64,8]{0,1:T(8,128)} %param.10) | copy-start | bytes 6148
  65.5 41.1 %copy-start.2 = (f32[8,8]{1,0:T(8,128)S(1)}, f32[8,8]{1,0:T(8,128)}, u32[]{:S(2)}) copy-start(f32[8,8]{1,0:T(8,128)} %tip_inverse.1) | copy-start | bytes 772
